TPU v7x, 512 devices: a whole 4x8x8 slice. The times are simulated.
512 devices in a mesh: coil: 8 (over z), slab: 64 (over y, x, core).
Axes of the slice: x: 4, y: 8, z: 8, core: 2. Of those that a mesh axis runs over, the one named last changes fastest.
Arguments:
- solution: float32 [2, 1, 128, 192, 256], P(None, None, 'slab', 'coil'), may hold values from -6 to 6
- residual: float32 [2, 1, 128, 192, 256], P(None, None, 'slab', 'coil'), may hold values from -6 to 6
- direction: float32 [2, 1, 128, 192, 256], P(None, None, 'slab', 'coil'), may hold values from -6 to 6
- sens_maps: float32 [2, 16, 128, 192, 256], P(None, 'coil', 'slab'), may hold values from -1.05 to 1.05
- sampling: int32 [1, 128, 192], replicated, may hold values from 0 to 1, as said below
Outputs:
- next_solution: float32 [2, 1, 128, 192, 256], P(None, None, 'slab', 'coil')
- next_residual: float32 [2, 1, 128, 192, 256], P(None, None, 'slab', 'coil')
- next_direction: float32 [2, 1, 128, 192, 256], P(None, None, 'slab', 'coil')
Inputs may be any that keep to these rules, and one draw needn't show every extreme that they name: sampling is 1 on every line whose kx lies within 4 of 0 or of 128 and whose ky lies within 4 of 0 or of 192.
All inputs are finite; a program needn't handle non-finite values.
Results may differ from a plain program's by a relative error of at most 0.00016.
Values sent between devices are 32-bit elements; how exact they have to be, the bound alone decides.
No kernel may reach another device: no remote copies, remote signals or barrier semaphores. Data moves between devices by JAX's collectives and lax.ppermute only.
A program may use at most 64 MiB of HBM per device.

v0:
```python
import math

import jax
import jax.numpy as jnp
from jax import lax
from jax.sharding import PartitionSpec as P

damping_weight = 0.5


def dft_table(length, inverse):
    index = jnp.arange(length, dtype=jnp.int32)
    phase = (index[:, None] * index[None, :] % length).astype(jnp.float32)
    angle = phase * (2.0 * math.pi / length)
    scale = 1.0 / math.sqrt(length)
    cosine = jnp.cos(angle) * scale
    sine = jnp.sin(angle) * scale
    if inverse:
        return jnp.stack([jnp.stack([cosine, -sine]), jnp.stack([sine, cosine])])
    return jnp.stack([jnp.stack([cosine, sine]), jnp.stack([-sine, cosine])])


def along_second(table, data):
    return jnp.einsum(
        "abky,bcfxyz->acfxkz",
        table,
        data,
        precision=lax.Precision.HIGHEST,
        preferred_element_type=jnp.float32,
    )


def front_first(table, data):
    return jnp.einsum(
        "abkx,wbcfxy->wacfky",
        table,
        data,
        precision=lax.Precision.HIGHEST,
        preferred_element_type=jnp.float32,
    )


def coil_product(maps, field):
    real_part = maps[0][:, None] * field[0][None] - maps[1][:, None] * field[1][None]
    imag_part = maps[0][:, None] * field[1][None] + maps[1][:, None] * field[0][None]
    return jnp.stack([real_part, imag_part])


def coil_combine(maps, data):
    real_part = jnp.sum(maps[0][:, None] * data[0] + maps[1][:, None] * data[1], axis=0)
    imag_part = jnp.sum(maps[0][:, None] * data[1] - maps[1][:, None] * data[0], axis=0)
    return jnp.stack([real_part, imag_part])


def front_mask(table_fwd, table_inv, weight, data):
    spectra = front_first(table_fwd, data)
    return front_first(table_inv, spectra * weight)


def readout_front(data, groups):
    shape = data.shape
    split = data.reshape(shape[:-1] + (groups, shape[-1] // groups))
    count = len(shape)
    return jnp.transpose(split, (count - 1, count) + tuple(range(count - 1)))


def readout_back(data):
    count = data.ndim
    moved = jnp.transpose(data, tuple(range(2, count)) + (0, 1))
    shape = moved.shape
    return moved.reshape(shape[:-2] + (shape[-2] * shape[-1],))


def body(solution, residual, direction, sens_maps, sampling):
    size_x = sampling.shape[1]
    size_y = sampling.shape[2]
    own_rows = direction.shape[3]
    groups = lax.axis_size("slab")
    first_fwd = dft_table(size_x, False)
    first_inv = dft_table(size_x, True)
    second_fwd = dft_table(size_y, False)
    second_inv = dft_table(size_y, True)
    weight = sampling.astype(jnp.float32)[None, None, None, :, :, :]
    gathered = lax.all_gather(direction, "coil", axis=3, tiled=True)
    coil_data = readout_front(along_second(second_fwd, coil_product(sens_maps, gathered)), groups)
    masked = front_mask(
        first_fwd,
        first_inv,
        weight,
        lax.all_to_all(coil_data, "slab", split_axis=0, concat_axis=5, tiled=True)[0],
    )
    returned = lax.all_to_all(masked[None], "slab", split_axis=5, concat_axis=0, tiled=True)
    partial_value = coil_combine(sens_maps, along_second(second_inv, readout_back(returned)))
    total = lax.psum(partial_value, "coil")
    offset = lax.axis_index("coil") * own_rows
    combined = lax.dynamic_slice_in_dim(total, offset, own_rows, 3)
    image_ap = combined + damping_weight * direction
    norm_now = lax.psum(jnp.sum(residual * residual), ("coil", "slab"))
    curvature = lax.psum(jnp.sum(direction * image_ap), ("coil", "slab"))
    alpha = norm_now / curvature
    next_residual = residual - alpha * image_ap
    fresh = lax.psum(jnp.sum(next_residual * next_residual), ("coil", "slab"))
    next_solution = solution + alpha * direction
    next_direction = next_residual + fresh / norm_now * direction
    return (next_solution, next_residual, next_direction)


def solution(mesh):
    in_specs = (
        P(None, None, "slab", "coil", None),
        P(None, None, "slab", "coil", None),
        P(None, None, "slab", "coil", None),
        P(None, "coil", "slab", None, None),
        P(),
    )
    out_specs = (
        P(None, None, "slab", "coil", None),
        P(None, None, "slab", "coil", None),
        P(None, None, "slab", "coil", None),
    )
    return jax.shard_map(body, mesh=mesh, in_specs=in_specs, out_specs=out_specs, check_vma=False)
```

profile of v0, /device:TPU:1, one launch (start us, length us, event | category | flops | bytes accessed | tf_op | source)
XLA Modules:
  0.0 470.8 jit_solution(7020334062249596251)
XLA Ops:
  7.2 0.8 sine_multiply_fusion
  8.0 0.8 fusion.44
  8.8 28.3 %all_gather.3 = f32[2,1,2,192,256]{4,3,2,1,0:T(8,128)S(1)} all-gather(f32[2,1,2,24,256]{4,3,2,1,0:T(8,128)} %param.7), channel_id=1, replica_groups=mesh['coil'=8,'slab'=64] {'coil'}, dimensions={3}, use_global_device_ids=true | all-gather | bytes 884736 | tf_op jit(solution)/shard_map/all_gather | solution.py:84
  37.1 0.0 copy-start
  37.1 0.1 slice_bitcast_fusion.3
  37.1 0.1 fusion.30
  37.3 1.2 copy-done
  38.5 0.2 fusion.20
  38.7 3.9 fusion.15
  42.6 2.8 copy.24
  45.4 2.7 copy.25
  48.1 16.0 %all-to-all-start = ((f32[64,4,2,2,1,2,192]{6,5,1,3,2,4,0:T(2,128)}), f32[64,4,2,2,1,2,192]{6,5,1,3,2,4,0:T(2,128)S(1)}, u32[]{:S(2)}, u32[]{:S(2)}) async-start(f32[64,4,2,2,1,2,192]{6,5,1,3,2,4,0:T(2,128)} %copy.25), calls=%async_computation | async-start | bytes 4194304 | tf_op jit(solution)/shard_map/all_to_all | solution.py:90
  64.1 0.2 all-reduce.3.cloned.1.call-start
  64.4 0.3 fusion.51
  64.6 0.3 sine_multiply_fusion.1
  65.0 0.9 convert_bitcast_fusion
  65.9 48.0 %all-to-all-done = f32[64,4,2,2,1,2,192]{6,5,1,3,2,4,0:T(2,128)S(1)} async-done(((f32[64,4,2,2,1,2,192]{6,5,1,3,2,4,0:T(2,128)}), f32[64,4,2,2,1,2,192]{6,5,1,3,2,4,0:T(2,128)S(1)}, u32[]{:S(2)}, u32[]{:S(2)}) %all-to-all-start) | async-done | bytes 1572896 | tf_op jit(solution)/shard_map/all_to_all | solution.py:90
  113.8 1.1 copy.26
  114.9 3.4 fusion
  118.3 2.6 fusion.12
  120.9 3.0 copy.28
  123.9 56.5 %all_to_all.33 = f32[1,4,2,2,1,128,192]{6,2,3,1,4,0,5:T(2,128)S(1)} all-to-all(f32[1,4,2,2,1,128,192]{6,2,3,1,4,0,5:T(2,128)S(1)} %copy.28), channel_id=1, replica_groups=mesh['coil'=8,'slab'=64] {'slab'}, dimensions={5} | all-to-all | bytes 3145728 | tf_op jit(solution)/shard_map/all_to_all | solution.py:92
  180.4 1.1 copy.29
  181.5 1.1 copy.30
  182.6 2.2 copy.31
  184.8 0.0 copy-start.1
  184.8 4.3 fusion.9
  189.1 0.0 copy-done.1
  189.1 0.3 fusion.23
  189.4 0.0 copy-start.3
  189.4 0.0 copy-start.2
  189.4 0.0 copy-start.5
  189.4 1.0 pad_maximum_fusion
  190.4 0.0 all-reduce.3.cloned.1.call-update
  190.4 0.0 copy-done.3
  190.4 0.6 multiply_reduce_fusion.2
  191.1 70.3 %all-reduce.3.cloned.1.call-done = f32[2,1,2,192,256]{4,3,2,1,0:T(8,128)} async-done(((f32[2,1,2,192,256]{4,3,2,1,0:T(8,128)}), f32[2,1,2,192,256]{4,3,2,1,0:T(8,128)}) %all-reduce.3.cloned.1.call-update) | async-done | bytes 786448 | tf_op jit(solution)/shard_map/psum | solution.py:94
  261.4 0.0 copy-done.2
  261.4 1.5 multiply_reduce_fusion.1
  262.9 101.4 %all-reduce = (f32[]{:T(128)}, f32[]{:T(128)}) all-reduce(f32[]{:T(128)} %multiply_reduce_fusion.2, f32[]{:T(128)} %multiply_reduce_fusion.1), channel_id=1, replica_groups=mesh['coil'=8,'slab'=64] {'coil','slab'}, use_global_device_ids=true, to_apply=%region_1.2 | all-reduce | flops 2 | bytes 16 | tf_op jit(solution)/shard_map/psum | solution.py:98
  365.6 1.5 multiply_reduce_fusion
  367.2 0.0 copy-start.4
  367.2 94.7 %psum.31 = f32[]{:T(128)} all-reduce(f32[]{:T(128)} %get-tuple-element.7), channel_id=1, replica_groups=mesh['coil'=8,'slab'=64] {'coil','slab'}, use_global_device_ids=true, to_apply=%region_8.9 | all-reduce | flops 1 | bytes 8 | tf_op jit(solution)/shard_map/psum | solution.py:102
  463.2 0.0 copy-done.5
  463.2 0.7 multiply_add_fusion
  463.9 0.0 copy-done.4
  (1 shorter events, 0.0 us)
Async XLA Ops:
  37.1 1.4 copy-start
  48.1 65.7 %all-to-all-start = ((f32[64,4,2,2,1,2,192]{6,5,1,3,2,4,0:T(2,128)}), f32[64,4,2,2,1,2,192]{6,5,1,3,2,4,0:T(2,128)S(1)}, u32[]{:S(2)}, u32[]{:S(2)}) async-start(f32[64,4,2,2,1,2,192]{6,5,1,3,2,4,0:T(2,128)} %copy.25), calls=%async_computation | async-start | bytes 4194304 | tf_op jit(solution)/shard_map/all_to_all | solution.py:90
  64.1 197.2 %all-reduce.3.cloned.1.call-start = ((), (), s32[]{:S(2)}) async-start(), calls=%async_computation.2 | async-start | bytes 1572864 | tf_op jit(solution)/shard_map/psum | solution.py:94
  184.8 4.3 copy-start.1
  189.4 1.0 copy-start.3
  189.4 72.0 %copy-start.2 = (f32[2,1,2,24,256]{4,3,2,1,0:T(8,128)S(1)}, f32[2,1,2,24,256]{4,3,2,1,0:T(8,128)}, u32[]{:S(2)}) copy-start(f32[2,1,2,24,256]{4,3,2,1,0:T(8,128)} %param.7) | copy-start | bytes 294916
  189.4 273.8 %copy-start.5 = (f32[2,1,2,24,256]{4,3,2,1,0:T(8,128)S(1)}, f32[2,1,2,24,256]{4,3,2,1,0:T(8,128)}, u32[]{:S(2)}) copy-start(f32[2,1,2,24,256]{4,3,2,1,0:T(8,128)} %param.5) | copy-start | bytes 294916
  367.2 96.8 %copy-start.4 = (f32[2,1,2,24,256]{4,3,2,1,0:T(8,128)}, f32[2,1,2,24,256]{4,3,2,1,0:T(8,128)S(1)}, u32[]{:S(2)}) copy-start(f32[2,1,2,24,256]{4,3,2,1,0:T(8,128)S(1)} %get-tuple-element.8) | copy-start | bytes 294916
Sparse Core Ops, SparseCore 0:
  190.5 70.7 all-reduce.2
where the time goes:
time: 471 us
  blocking collectives  281 us (60%)
  waiting for transfers between devices  118 us (25%)
  between operations  16.9 us (4%)
  starting transfers between devices  16.2 us (3%)
  local copies, waits for them, and re-layouts  15.2 us (3%)
  matrix products  14.2 us (3%)
  other arithmetic  9.03 us (2%)
    psum x1, blocking collectives, body(): norm_now = lax.psum(jnp.sum(residual * residual), ('coil', 'slab'))  101 us
    psum x1, blocking collectives, body(): fresh = lax.psum(jnp.sum(next_residual * next_residual), ('coil', 'slab'))  94.7 us
    psum x1, waiting for transfers between devices, body(): total = lax.psum(partial_value, 'coil')  70.3 us
    all_to_all x1, blocking collectives, body(): lax.all_to_all(masked[None], 'slab', split_axis=5, concat_axis=0, tiled=T...  56.5 us
    all_to_all x1, waiting for transfers between devices, body(): lax.all_to_all(coil_data, 'slab', split_axis=0, concat_axis=5, tiled=True)  48 us
    all_gather x1, blocking collectives, body(): gathered = lax.all_gather(direction, 'coil', axis=3, tiled=True)  28.3 us
    all_to_all x1, starting transfers between devices, body(): lax.all_to_all(coil_data, 'slab', split_axis=0, concat_axis=5, tiled=True)  16 us
  transfers between devices with their start and end apart: 2, of which 2 were waited for; matrix products, arithmetic and copies ran while one was open for 0% of the time, Pallas kernels for 0%

commit v1 on v0

v1 whole, which is shorter than its diff:
```python
import math

import jax
import jax.numpy as jnp
import ml_dtypes
import numpy as np
from jax import lax
from jax.experimental import pallas as pl
from jax.experimental.pallas import tpu as pltpu
from jax.sharding import PartitionSpec as P

damping_weight = 0.5

LANES = 128
ROWS = 8
MESSAGE_D = 6
MESSAGE_R = 7
HALF = 64
SUMS_AT = 48


def split_pair(table):
    high = table.astype(ml_dtypes.bfloat16)
    low = (table - high.astype(np.float64)).astype(ml_dtypes.bfloat16)
    return np.stack([high, low])


def angles(length):
    index = np.arange(length)
    angle = (index[:, None] * index[None, :] % length) * (2.0 * math.pi / length)
    scale = 1.0 / math.sqrt(length)
    return np.cos(angle) * scale, np.sin(angle) * scale


def make_tables(size_x, size_y):
    cos_y, sin_y = angles(size_y)
    cos_x, sin_x = angles(size_x)
    re_from_re = np.concatenate([cos_y[:, :LANES], -sin_y[:, :LANES], cos_y[:, LANES:], -sin_y[:, LANES:]], axis=1)
    re_from_im = np.concatenate([sin_y[:, :LANES], cos_y[:, :LANES], sin_y[:, LANES:], cos_y[:, LANES:]], axis=1)
    fwd_y = np.zeros((2, 4 * LANES, 3 * LANES))
    for row in range(2):
        for part, block in enumerate((re_from_re, re_from_im)):
            base = part * 2 * LANES
            fwd_y[row, base : base + LANES] = block[:LANES]
            high = base + LANES + row * HALF
            fwd_y[row, high : high + HALF] = block[LANES:]
    to_re = np.concatenate([cos_y[:LANES], -sin_y[:LANES], cos_y[LANES:], -sin_y[LANES:]], axis=0)
    to_im = np.concatenate([sin_y[:LANES], cos_y[:LANES], sin_y[LANES:], cos_y[LANES:]], axis=0)
    inv_low = np.concatenate([to_re[:, :LANES], to_im[:, :LANES]], axis=1)
    inv_high = np.zeros((2, 3 * LANES, 2 * LANES))
    for row in range(2):
        inv_high[row, :, row * HALF : (row + 1) * HALF] = to_re[:, LANES:]
        inv_high[row, :, LANES + row * HALF : LANES + (row + 1) * HALF] = to_im[:, LANES:]
    order = np.concatenate([np.arange(0, size_x, 2), np.arange(1, size_x, 2)])
    fwd_x = np.concatenate([cos_x[:, order], sin_x[:, order]], axis=0)
    inv_x = np.concatenate([cos_x[order], sin_x[order]], axis=0)
    return [split_pair(t) for t in (fwd_y, fwd_x, inv_x, inv_low, inv_high)]


def pack_kernel(maps_ref, direction_ref, residual_ref, out_ref):
    cells = maps_ref.shape[4]

    def put(core, slot, block):
        out_ref[pl.ds(core * ROWS + slot, cells, stride=2 * ROWS), :] = block.T

    for core in range(2):
        for part in range(2):
            for row in range(2):
                put(core, part * 2 + row, maps_ref[part, core, row, :LANES, :])
            put(
                core,
                4 + part,
                jnp.concatenate([maps_ref[part, core, 0, LANES:, :], maps_ref[part, core, 1, LANES:, :]], axis=0),
            )
    own = direction_ref.shape[3]
    pieces = [direction_ref[part, 0, row] for part in range(2) for row in range(2)]
    filler = jnp.zeros((LANES - 4 * own, cells), jnp.float32)
    field = jnp.concatenate(pieces + [filler], axis=0)
    for core in range(2):
        put(core, MESSAGE_D, field)
        filler = jnp.zeros((LANES - 2 * own, cells), jnp.float32)
        put(core, MESSAGE_R, jnp.concatenate([residual_ref[core, 0, 0], residual_ref[core, 0, 1], filler], axis=0))


def lane_index(rows):
    return lax.broadcasted_iota(jnp.int32, (rows, LANES), 1)


def spread(blocks, own, slots):
    lane = lane_index(HALF)
    result = []
    for slot in slots:
        low = jnp.zeros((HALF, LANES), jnp.float32)
        high = jnp.zeros((HALF, LANES), jnp.float32)
        for c, block in enumerate(blocks):
            start = c * own
            moved = pltpu.roll(block, (start - slot * own) % LANES, 1)
            if start < LANES:
                low = jnp.where((lane >= start) & (lane < start + own), moved, low)
            if start + own > LANES:
                at = start - LANES
                high = jnp.where((lane >= at) & (lane < at + own), moved, high)
        result.append((low, high))
    return result


def join_high(first, second):
    return jnp.where(lane_index(HALF) < HALF, first, pltpu.roll(second, HALF, 1))


def halves(value):
    high = value.astype(jnp.bfloat16)
    low = (value - high.astype(jnp.float32)).astype(jnp.bfloat16)
    return high, low


def dot3(left_high, left_low, right_high, right_low):
    def dot(a, b):
        return jnp.dot(a, b, preferred_element_type=jnp.float32)

    return dot(left_high, right_high) + (dot(left_high, right_low) + dot(left_low, right_high))


def normal_kernel(
    core_ref,
    recv_ref,
    weight_ref,
    fwd_y_ref,
    fwd_x_ref,
    inv_x_ref,
    inv_low_ref,
    inv_high_ref,
    own_ref,
    send_ref,
    field_ref,
    line_ref,
    mid_ref,
    back_ref,
    total_ref,
    image_ref,
):
    coils = recv_ref.shape[0] // (ROWS * HALF)
    own = 2 * 96 // coils

    def load(c, slot):
        return recv_ref[pl.ds(c * HALF * ROWS + slot, HALF, stride=ROWS), :]

    pieces = spread([load(c, MESSAGE_D) for c in range(coils)], own, range(4))
    for part in range(2):
        (low0, high0), (low1, high1) = pieces[2 * part], pieces[2 * part + 1]
        image_ref[part, 0] = low0
        image_ref[part, 1] = low1
        image_ref[part, 2] = join_high(high0, high1)
    for c in range(coils):
        rows = pl.ds(c * HALF, HALF)
        for slot in range(3):
            s_re = load(c, slot if slot < 2 else 4)
            s_im = load(c, slot + 2 if slot < 2 else 5)
            d_re, d_im = image_ref[0, slot], image_ref[1, slot]
            for part, value in enumerate((s_re * d_re - s_im * d_im, s_re * d_im + s_im * d_re)):
                base = part * 2 * LANES
                for term, half in enumerate(halves(value)):
                    if slot < 2:
                        line_ref[term, slot, rows, base : base + LANES] = half
                    else:
                        for row in range(2):
                            line_ref[term, row, rows, base + LANES : base + 2 * LANES] = half
    for row in range(2):
        spectra = dot3(line_ref[0, row], line_ref[1, row], fwd_y_ref[0, row], fwd_y_ref[1, row])
        for term, half in enumerate(halves(spectra)):
            for c in range(coils):
                mid_ref[term, c, row * HALF : (row + 1) * HALF, :] = half[c * HALF : (c + 1) * HALF]
    weight_low = weight_ref[:, :LANES].astype(jnp.float32)
    weight_high = weight_ref[:, LANES:].astype(jnp.float32)
    weight_mix = jnp.concatenate([weight_high, weight_high], axis=1)
    sign = jnp.where(lane_index(LANES) < HALF, 1.0, -1.0).astype(jnp.float32)
    for c in range(coils):
        both = dot3(fwd_x_ref[0], fwd_x_ref[1], mid_ref[0, c], mid_ref[1, c])
        p, q = both[:LANES], both[LANES:]
        turned = sign * pltpu.roll(q[:, 2 * LANES :], HALF, 1)
        masked = jnp.concatenate(
            [
                (p[:, :LANES] + q[:, LANES : 2 * LANES]) * weight_low,
                (p[:, LANES : 2 * LANES] - q[:, :LANES]) * weight_low,
                (p[:, 2 * LANES :] + turned) * weight_mix,
            ],
            axis=1,
        )
        masked_high, masked_low = halves(masked)
        both = dot3(inv_x_ref[0], inv_x_ref[1], masked_high, masked_low)
        p, q = both[:LANES], both[LANES:]
        turned = sign * pltpu.roll(q[:, 2 * LANES :], HALF, 1)
        columns = (
            p[:, :LANES] - q[:, LANES : 2 * LANES],
            p[:, LANES : 2 * LANES] + q[:, :LANES],
            p[:, 2 * LANES :] - turned,
        )
        for group, value in enumerate(columns):
            for term, half in enumerate(halves(value)):
                for row in range(2):
                    back_ref[term, row, c * HALF : (c + 1) * HALF, group * LANES : (group + 1) * LANES] = half[
                        row * HALF : (row + 1) * HALF
                    ]
    for slot in range(3):
        if slot < 2:
            value = dot3(back_ref[0, slot], back_ref[1, slot], inv_low_ref[0], inv_low_ref[1])
        else:
            value = dot3(back_ref[0, 0], back_ref[1, 0], inv_high_ref[0, 0], inv_high_ref[1, 0]) + dot3(
                back_ref[0, 1], back_ref[1, 1], inv_high_ref[0, 1], inv_high_ref[1, 1]
            )
        sum_re = jnp.zeros((HALF, LANES), jnp.float32)
        sum_im = jnp.zeros((HALF, LANES), jnp.float32)
        for c in range(coils):
            s_re = load(c, slot if slot < 2 else 4)
            s_im = load(c, slot + 2 if slot < 2 else 5)
            y_re = value[c * HALF : (c + 1) * HALF, :LANES]
            y_im = value[c * HALF : (c + 1) * HALF, LANES:]
            sum_re = sum_re + (s_re * y_re + s_im * y_im)
            sum_im = sum_im + (s_re * y_im - s_im * y_re)
        total_ref[0, slot] = sum_re
        total_ref[1, slot] = sum_im
    core = core_ref[0]
    own_ref[...] = total_ref[core]
    send_ref[...] = total_ref[1 - core]
    field_ref[0] = image_ref[core]
    pieces = spread([load(c, MESSAGE_R) for c in range(coils)], own, range(2))
    field_ref[1, 0] = pieces[0][0]
    field_ref[1, 1] = pieces[1][0]
    field_ref[1, 2] = join_high(pieces[0][1], pieces[1][1])


def finish_kernel(own_ref, other_ref, field_ref, out_ref):
    direction = field_ref[0]
    residual = field_ref[1]
    image_ap = own_ref[...] + other_ref[...] + damping_weight * direction
    lane = lane_index(HALF)
    coils = out_ref.shape[0] // HALF
    own = 2 * 96 // coils
    sums = jnp.zeros((HALF, LANES), jnp.float32)
    products = (residual * residual, direction * image_ap, residual * image_ap, image_ap * image_ap)
    for index, product in enumerate(products):
        sums = jnp.where(lane == SUMS_AT + index, jnp.sum(product), sums)
    high = image_ap[2]
    for c in range(coils):
        start = c * own
        block = sums
        for row in range(2):
            at = row * own
            inside = (lane >= at) & (lane < at + own)
            if start < LANES:
                block = jnp.where(inside, pltpu.roll(image_ap[row], (at - start) % LANES, 1), block)
            if start + own > LANES:
                moved = pltpu.roll(high, (at - (start - LANES + row * HALF)) % LANES, 1)
                if start < LANES:
                    inside = inside & (lane >= at + LANES - start)
                block = jnp.where(inside, moved, block)
        out_ref[c * HALF : (c + 1) * HALF, :] = block


def update_kernel(
    recv_ref, solution_ref, residual_ref, direction_ref, next_solution_ref, next_residual_ref, next_direction_ref
):
    cells = recv_ref.shape[0] // 2
    own = direction_ref.shape[3]
    totals = jnp.sum(recv_ref[...], axis=0, keepdims=True)
    lane = lax.broadcasted_iota(jnp.int32, (1, LANES), 1)

    def pick(index):
        return jnp.sum(jnp.where(lane == SUMS_AT + index, totals, 0.0), axis=1, keepdims=True)

    norm_now, curvature, cross, square = pick(0), pick(1), pick(2), pick(3)
    alpha = norm_now / curvature
    fresh = jnp.maximum(norm_now + alpha * (alpha * square - 2.0 * cross), 0.0)
    beta = fresh / norm_now
    for part in range(2):
        turned = recv_ref[pl.ds(part, cells, stride=2), :].T
        for row in range(2):
            image_ap = turned[row * own : (row + 1) * own]
            direction = direction_ref[part, 0, row]
            next_residual = residual_ref[part, 0, row] - alpha * image_ap
            next_solution_ref[part, 0, row] = solution_ref[part, 0, row] + alpha * direction
            next_residual_ref[part, 0, row] = next_residual
            next_direction_ref[part, 0, row] = next_residual + beta * direction


def body(solution, residual, direction, sens_maps, sampling):
    axes = ("coil", "slab")
    devices = lax.axis_size(axes)
    planes = lax.axis_size("coil")
    f32 = jnp.float32
    params = pltpu.CompilerParams(vmem_limit_bytes=48 * 1024 * 1024)
    packed = pl.pallas_call(
        pack_kernel,
        out_shape=jax.ShapeDtypeStruct((devices * ROWS, LANES), f32),
        compiler_params=params,
        name="pack",
    )(sens_maps, direction, residual)
    moved = lax.all_to_all(packed.reshape(devices, ROWS, LANES), axes, 0, 0, tiled=True)
    tables = [jnp.asarray(t) for t in make_tables(sampling.shape[1], sampling.shape[2])]
    core = (lax.axis_index("slab") % 2).astype(jnp.int32).reshape(1)
    lines = planes * HALF
    bf16 = jnp.bfloat16
    whole = pl.BlockSpec(memory_space=pltpu.VMEM)
    part = jax.ShapeDtypeStruct((3, HALF, LANES), f32)
    own, send, field = pl.pallas_call(
        normal_kernel,
        in_specs=[pl.BlockSpec(memory_space=pltpu.SMEM)] + [whole] * 7,
        out_shape=(part, part, jax.ShapeDtypeStruct((2, 3, HALF, LANES), f32)),
        scratch_shapes=[
            pltpu.VMEM((2, 2, lines, 4 * LANES), bf16),
            pltpu.VMEM((2, planes, LANES, 3 * LANES), bf16),
            pltpu.VMEM((2, 2, lines, 3 * LANES), bf16),
            pltpu.VMEM((2, 3, HALF, LANES), f32),
            pltpu.VMEM((2, 3, HALF, LANES), f32),
        ],
        compiler_params=params,
        name="normal",
    )(core, moved.reshape(devices * ROWS, LANES), sampling[0], *tables)
    swap = [(i, i ^ 1) for i in range(lax.axis_size("slab"))]
    other = lax.ppermute(send, "slab", swap)
    result = pl.pallas_call(
        finish_kernel,
        out_shape=jax.ShapeDtypeStruct((devices, LANES), f32),
        compiler_params=params,
        name="finish",
    )(own, other, field)
    home = lax.all_to_all(result.reshape(devices, 1, LANES), axes, 0, 0, tiled=True).reshape(devices, LANES)
    out = jax.ShapeDtypeStruct(direction.shape, f32)
    return tuple(
        pl.pallas_call(update_kernel, out_shape=(out, out, out), compiler_params=params, name="update")(
            home, solution, residual, direction
        )
    )


def solution(mesh):
    image = P(None, None, "slab", "coil", None)
    in_specs = (image, image, image, P(None, "coil", "slab", None, None), P())
    return jax.shard_map(body, mesh=mesh, in_specs=in_specs, out_specs=(image, image, image), check_vma=False)
```

time: 471 us -> 126 us (0.27)
  blocking collectives: 281 us -> 26.7 us
  waiting for transfers between devices: 118 us -> 53.9 us
  between operations: 16.9 us -> 0.73 us
  matrix products: 14.2 us -> 0 us
  Pallas kernels: 0 us -> 10.5 us
  starting transfers between devices: 16.2 us -> 25.7 us
  other arithmetic: 9.03 us -> 0 us
  local copies, waits for them, and re-layouts: 15.2 us -> 7.84 us
    psum x2 -> x0, blocking collectives: 196 us -> none  [the longest x1 101 us: body(): norm_now = lax.psum(jnp.sum(residual * residual), ('coil', 'slab'))]
    psum x1 -> x0, waiting for transfers between devices: 70.3 us -> none  [body(): total = lax.psum(partial_value, 'coil')]
    all_to_all x1, blocking collectives: 56.5 us -> 26.7 us  [body(): lax.all_to_all(result.reshape(devices, 1, LANES), axes, 0, 0, tiled=True)]
    all_gather x1 -> x0, blocking collectives: 28.3 us -> none  [body(): gathered = lax.all_gather(direction, 'coil', axis=3, tiled=True)]
    dot_general x4 -> x0, matrix products: 14.2 us -> none  [the longest x2 8.19 us: along_second(): jnp.einsum('abky,bcfxyz->acfxkz', table, data, precision=lax.Precision.HI...]
    pallas_call x0 -> x4, Pallas kernels: none -> 10.5 us  [the longest x1 8.29 us: body(): pl.pallas_call(normal_kernel, in_specs=[pl.BlockSpec(memory_space=pltpu.S...]
    unnamed x12 -> x25, local copies, waits for them, and re-layouts: 1.27 us -> 7.84 us
    transpose x3 -> x0, local copies, waits for them, and re-layouts: 6.53 us -> none  [the longest x1 2.77 us: along_second(): jnp.einsum('abky,bcfxyz->acfxkz', table, data, precision=lax.Precision.HI...]
  transfers between devices with their start and end apart: 2 -> 2, of which waited for: 2 -> 2; matrix products, arithmetic and copies ran while one was open for 0% -> 1% of each run, Pallas kernels for 0% -> 0%
where the time goes in v1:
time: 126 us; the launch traced here: 125 us
  waiting for transfers between devices  53.9 us (43%)
  blocking collectives  26.7 us (21%)
  starting transfers between devices  25.7 us (20%)
  Pallas kernels  10.5 us (8%)
  local copies, waits for them, and re-layouts  7.84 us (6%)
    all_to_all x1, waiting for transfers between devices, body(): lax.all_to_all(packed.reshape(devices, ROWS, LANES), axes, 0, 0, tiled=True)  53 us
    all_to_all x1, blocking collectives, body(): lax.all_to_all(result.reshape(devices, 1, LANES), axes, 0, 0, tiled=True)  26.7 us
    all_to_all x1, starting transfers between devices, body(): lax.all_to_all(packed.reshape(devices, ROWS, LANES), axes, 0, 0, tiled=True)  22.2 us
    pallas_call x1, Pallas kernels, body(): pl.pallas_call(normal_kernel, in_specs=[pl.BlockSpec(memory_space=pltpu.S...  8.29 us
    unnamed x25, local copies, waits for them, and re-layouts  7.84 us
    ppermute x1, starting transfers between devices, body(): other = lax.ppermute(send, 'slab', swap)  3.53 us
  transfers between devices with their start and end apart: 2, of which 2 were waited for; matrix products, arithmetic and copies ran while one was open for 1% of the time, Pallas kernels for 0%

profile of v1, /device:TPU:1, one launch (start us, length us, event | category | flops | bytes accessed | tf_op | source)
XLA Modules:
  0.0 125.4 jit_solution(12984831832519703353)
XLA Ops:
  0.6 0.0 copy-start.1
  0.6 1.4 %copy-done.1 = f32[2,2,2,192,256]{4,3,2,1,0:T(8,128)S(1)} copy-done((f32[2,2,2,192,256]{4,3,2,1,0:T(8,128)S(1)}, f32[2,2,2,192,256]{4,3,2,1,0:T(8,128)}, u32[]{:S(2)}) %copy-start.1) | copy-done | bytes 1572888
  2.0 0.0 copy-start.5
  2.0 0.9 copy-done.5
  2.9 0.0 copy-start.7
  2.9 0.9 copy-done.7
  3.8 1.1 pack.1
  4.9 0.0 copy-start
  5.0 1.3 %copy-done = f32[4096,128]{1,0:T(8,128)} copy-done((f32[4096,128]{1,0:T(8,128)}, f32[4096,128]{1,0:T(8,128)S(1)}, u32[]{:S(2)}) %copy-start) | copy-done | bytes 2097176
  6.3 0.0 copy-start.3
  6.3 0.0 copy-start.4
  6.3 0.0 copy-start.9
  6.3 22.2 %all-to-all-start = ((f32[512,8,128]{2,1,0:T(8,128)}), f32[512,8,128]{2,1,0:T(8,128)S(1)}, u32[]{:S(2)}, u32[]{:S(2)}) async-start(f32[512,8,128]{2,1,0:T(8,128)} %bitcast.9), calls=%async_computation | async-start | bytes 4194304 | tf_op jit(solution)/shard_map/all_to_all | solution.py:298
  28.5 1.0 copy.14
  29.5 53.0 %all-to-all-done = f32[512,8,128]{2,1,0:T(8,128)S(1)} async-done(((f32[512,8,128]{2,1,0:T(8,128)}), f32[512,8,128]{2,1,0:T(8,128)S(1)}, u32[]{:S(2)}, u32[]{:S(2)}) %all-to-all-start) | async-done | bytes 2097184 | tf_op jit(solution)/shard_map/all_to_all | solution.py:298
  82.5 0.0 copy-done.3
  82.5 0.0 copy-done.4
  82.5 0.0 copy-done.9
  82.5 0.0 copy-start.2
  82.5 1.4 %copy-done.2 = bf16[2,2,512,384]{3,2,1,0:T(8,128)(2,1)S(1)} copy-done((bf16[2,2,512,384]{3,2,1,0:T(8,128)(2,1)S(1)}, bf16[2,2,512,384]{3,2,1,0:T(8,128)(2,1)}, u32[]{:S(2)}) %copy-start.2) | copy-done | bytes 1572888
  83.9 0.0 copy-start.10
  83.9 0.9 copy-done.10
  84.8 0.0 copy-start.6
  84.8 0.0 copy-start.8
  84.8 0.0 copy-start.11
  84.8 8.3 %normal.1 = (f32[3,64,128]{2,1,0:T(8,128)S(1)}, f32[3,64,128]{2,1,0:T(8,128)S(1)}, f32[2,3,64,128]{3,2,1,0:T(8,128)S(1)}) custom-call(s32[1]{0:T(128)} %bitcast.core_ref, f32[4096,128]{1,0:T(8,128)S(1)} %bitcast.8, s32[128,192]{1,0:T(8,128)S(1)} %bitcast.12, bf16[2,2,512,384]{3,2,1,0:T(8,128)(2,1)S(1)} %copy-done.2, bf16[2,256,128]{2,1,0:T(8,128)(2,1)S(1)} %copy-done.9, ...), custom_call_target="tpu_custom_call" | custom-call | tf_op jit(solution)/shard_map/normal/pallas_call | solution.py:305
  93.1 3.5 %collective-permute-start = (f32[3,64,128]{2,1,0:T(8,128)S(1)}, f32[3,64,128]{2,1,0:T(8,128)S(1)}, u32[]{:S(2)}, u32[]{:S(2)}) collective-permute-start(f32[3,64,128]{2,1,0:T(8,128)S(1)} %get-tuple-element.7), channel_id=1, source_target_pairs={{0,1},{1,0},{2,3},{3,2},{4,5},{5,4},{6,7},{7,6},{8,9},{9,8},{10,11... | collective-permute-start | bytes 294920 | tf_op jit(solution)/shard_map/ppermute | solution.py:320
  96.6 0.9 collective-permute-done.other_ref
  97.6 0.3 finish.1
  97.8 26.7 %all_to_all.10 = f32[512,1,128]{2,1,0:T(1,128)S(1)} all-to-all(f32[512,1,128]{2,1,0:T(1,128)S(1)} %bitcast.11), channel_id=1, replica_groups=mesh['coil'=8,'slab'=64] {'coil','slab'}, dimensions={0} | all-to-all | bytes 524288 | tf_op jit(solution)/shard_map/all_to_all | solution.py:327
  124.5 0.0 copy-done.6
  124.5 0.0 copy-done.8
  124.5 0.0 copy-done.11
  124.5 0.9 update.1
Async XLA Ops:
  0.6 1.4 %copy-start.1 = (f32[2,2,2,192,256]{4,3,2,1,0:T(8,128)S(1)}, f32[2,2,2,192,256]{4,3,2,1,0:T(8,128)}, u32[]{:S(2)}) copy-start(f32[2,2,2,192,256]{4,3,2,1,0:T(8,128)} %maps_ref.1) | copy-start | bytes 4718596
  2.0 0.9 copy-start.5
  2.9 0.9 copy-start.7
  4.9 1.3 %copy-start = (f32[4096,128]{1,0:T(8,128)}, f32[4096,128]{1,0:T(8,128)S(1)}, u32[]{:S(2)}) copy-start(f32[4096,128]{1,0:T(8,128)S(1)} %pack.1) | copy-start | bytes 6291460
  6.3 76.2 %copy-start.3 = (bf16[2,2,384,256]{3,2,1,0:T(8,128)(2,1)S(1)}, bf16[2,2,384,256]{3,2,1,0:T(8,128)(2,1)}, u32[]{:S(2)}) copy-start(bf16[2,2,384,256]{3,2,1,0:T(8,128)(2,1)} %constant.31.clone.inv_high_ref) | copy-start | bytes 2359300
  6.3 76.2 %copy-start.4 = (bf16[2,384,256]{2,1,0:T(8,128)(2,1)S(1)}, bf16[2,384,256]{2,1,0:T(8,128)(2,1)}, u32[]{:S(2)}) copy-start(bf16[2,384,256]{2,1,0:T(8,128)(2,1)} %constant.30.clone.inv_low_ref) | copy-start | bytes 1179652
  6.3 76.2 %copy-start.9 = (bf16[2,256,128]{2,1,0:T(8,128)(2,1)S(1)}, bf16[2,256,128]{2,1,0:T(8,128)(2,1)}, u32[]{:S(2)}) copy-start(bf16[2,256,128]{2,1,0:T(8,128)(2,1)} %constant.28.clone.fwd_x_ref) | copy-start | bytes 393220
  6.3 76.2 %all-to-all-start = ((f32[512,8,128]{2,1,0:T(8,128)}), f32[512,8,128]{2,1,0:T(8,128)S(1)}, u32[]{:S(2)}, u32[]{:S(2)}) async-start(f32[512,8,128]{2,1,0:T(8,128)} %bitcast.9), calls=%async_computation | async-start | bytes 4194304 | tf_op jit(solution)/shard_map/all_to_all | solution.py:298
  82.5 1.4 %copy-start.2 = (bf16[2,2,512,384]{3,2,1,0:T(8,128)(2,1)S(1)}, bf16[2,2,512,384]{3,2,1,0:T(8,128)(2,1)}, u32[]{:S(2)}) copy-start(bf16[2,2,512,384]{3,2,1,0:T(8,128)(2,1)} %constant.27.clone.fwd_y_ref) | copy-start | bytes 4718596
  83.9 0.9 copy-start.10
  84.8 39.7 %copy-start.6 = (f32[2,1,2,24,256]{4,3,2,1,0:T(8,128)S(1)}, f32[2,1,2,24,256]{4,3,2,1,0:T(8,128)}, u32[]{:S(2)}) copy-start(f32[2,1,2,24,256]{4,3,2,1,0:T(8,128)} %direction_ref.3) | copy-start | bytes 294916
  84.8 39.7 %copy-start.8 = (f32[2,1,2,24,256]{4,3,2,1,0:T(8,128)S(1)}, f32[2,1,2,24,256]{4,3,2,1,0:T(8,128)}, u32[]{:S(2)}) copy-start(f32[2,1,2,24,256]{4,3,2,1,0:T(8,128)} %residual_ref.3) | copy-start | bytes 294916
  84.8 39.7 %copy-start.11 = (f32[2,1,2,24,256]{4,3,2,1,0:T(8,128)S(1)}, f32[2,1,2,24,256]{4,3,2,1,0:T(8,128)}, u32[]{:S(2)}) copy-start(f32[2,1,2,24,256]{4,3,2,1,0:T(8,128)} %solution_ref.1) | copy-start | bytes 294916
  93.1 4.5 %collective-permute-start = (f32[3,64,128]{2,1,0:T(8,128)S(1)}, f32[3,64,128]{2,1,0:T(8,128)S(1)}, u32[]{:S(2)}, u32[]{:S(2)}) collective-permute-start(f32[3,64,128]{2,1,0:T(8,128)S(1)} %get-tuple-element.7), channel_id=1, source_target_pairs={{0,1},{1,0},{2,3},{3,2},{4,5},{5,4},{6,7},{7,6},{8,9},{9,8},{10,11... | collective-permute-start | bytes 294920 | tf_op jit(solution)/shard_map/ppermute | solution.py:320

commit v2 on v1

--- a/solution.py
+++ b/solution.py
@@ -37,41 +37,32 @@
     cos_x, sin_x = angles(size_x)
     re_from_re = np.concatenate([cos_y[:, :LANES], -sin_y[:, :LANES], cos_y[:, LANES:], -sin_y[:, LANES:]], axis=1)
     re_from_im = np.concatenate([sin_y[:, :LANES], cos_y[:, :LANES], sin_y[:, LANES:], cos_y[:, LANES:]], axis=1)
-    fwd_y = np.zeros((2, 4 * LANES, 3 * LANES))
-    for row in range(2):
-        for part, block in enumerate((re_from_re, re_from_im)):
-            base = part * 2 * LANES
-            fwd_y[row, base : base + LANES] = block[:LANES]
-            high = base + LANES + row * HALF
-            fwd_y[row, high : high + HALF] = block[LANES:]
-    to_re = np.concatenate([cos_y[:LANES], -sin_y[:LANES], cos_y[LANES:], -sin_y[LANES:]], axis=0)
-    to_im = np.concatenate([sin_y[:LANES], cos_y[:LANES], sin_y[LANES:], cos_y[LANES:]], axis=0)
-    inv_low = np.concatenate([to_re[:, :LANES], to_im[:, :LANES]], axis=1)
-    inv_high = np.zeros((2, 3 * LANES, 2 * LANES))
-    for row in range(2):
-        inv_high[row, :, row * HALF : (row + 1) * HALF] = to_re[:, LANES:]
-        inv_high[row, :, LANES + row * HALF : LANES + (row + 1) * HALF] = to_im[:, LANES:]
+    fwd_y = np.concatenate([re_from_re[:LANES], re_from_im[:LANES], re_from_re[LANES:], re_from_im[LANES:]], axis=0)
     order = np.concatenate([np.arange(0, size_x, 2), np.arange(1, size_x, 2)])
     fwd_x = np.concatenate([cos_x[:, order], sin_x[:, order]], axis=0)
     inv_x = np.concatenate([cos_x[order], sin_x[order]], axis=0)
-    return [split_pair(t) for t in (fwd_y, fwd_x, inv_x, inv_low, inv_high)]
-
-
-def pack_kernel(maps_ref, direction_ref, residual_ref, out_ref):
+    return [split_pair(t) for t in (fwd_y, fwd_y.T, fwd_x, inv_x)]
+
+
+def pack_kernel(maps_hbm, direction_hbm, residual_hbm, out_ref, maps_ref, direction_ref, residual_ref, maps_sem, image_sem):
     cells = maps_ref.shape[4]
+    copies = [
+        pltpu.make_async_copy(maps_hbm.at[part, core], maps_ref.at[part, core], maps_sem.at[part, core])
+        for core in range(2)
+        for part in range(2)
+    ]
+    images = [
+        pltpu.make_async_copy(direction_hbm, direction_ref, image_sem.at[0]),
+        pltpu.make_async_copy(residual_hbm, residual_ref, image_sem.at[1]),
+    ]
+    for copy in images + copies:
+        copy.start()
 
     def put(core, slot, block):
         out_ref[pl.ds(core * ROWS + slot, cells, stride=2 * ROWS), :] = block.T
 
-    for core in range(2):
-        for part in range(2):
-            for row in range(2):
-                put(core, part * 2 + row, maps_ref[part, core, row, :LANES, :])
-            put(
-                core,
-                4 + part,
-                jnp.concatenate([maps_ref[part, core, 0, LANES:, :], maps_ref[part, core, 1, LANES:, :]], axis=0),
-            )
+    for copy in images:
+        copy.wait()
     own = direction_ref.shape[3]
     pieces = [direction_ref[part, 0, row] for part in range(2) for row in range(2)]
     filler = jnp.zeros((LANES - 4 * own, cells), jnp.float32)
@@ -80,6 +71,16 @@
         put(core, MESSAGE_D, field)
         filler = jnp.zeros((LANES - 2 * own, cells), jnp.float32)
         put(core, MESSAGE_R, jnp.concatenate([residual_ref[core, 0, 0], residual_ref[core, 0, 1], filler], axis=0))
+    for core in range(2):
+        for part in range(2):
+            copies[core * 2 + part].wait()
+            for row in range(2):
+                put(core, part * 2 + row, maps_ref[part, core, row, :LANES, :])
+            put(
+                core,
+                4 + part,
+                jnp.concatenate([maps_ref[part, core, 0, LANES:, :], maps_ref[part, core, 1, LANES:, :]], axis=0),
+            )
 
 
 def lane_index(rows):
@@ -104,8 +105,12 @@
     return result
 
 
+def join_low(first, second):
+    return jnp.where(lane_index(HALF) < HALF, first, pltpu.roll(second, HALF, 1))
+
+
 def join_high(first, second):
-    return jnp.where(lane_index(HALF) < HALF, first, pltpu.roll(second, HALF, 1))
+    return jnp.where(lane_index(HALF) < HALF, pltpu.roll(first, HALF, 1), second)
 
 
 def halves(value):
@@ -126,16 +131,14 @@
     recv_ref,
     weight_ref,
     fwd_y_ref,
+    inv_y_ref,
     fwd_x_ref,
     inv_x_ref,
-    inv_low_ref,
-    inv_high_ref,
     own_ref,
     send_ref,
     field_ref,
     line_ref,
     mid_ref,
-    back_ref,
     total_ref,
     image_ref,
 ):
@@ -150,28 +153,32 @@
         (low0, high0), (low1, high1) = pieces[2 * part], pieces[2 * part + 1]
         image_ref[part, 0] = low0
         image_ref[part, 1] = low1
-        image_ref[part, 2] = join_high(high0, high1)
+        image_ref[part, 2] = join_low(high0, high1)
+
+    def store_line(row, c, column, value):
+        for term, half in enumerate(halves(value)):
+            line_ref[term, row, c * HALF : (c + 1) * HALF, column * LANES : (column + 1) * LANES] = half
+
     for c in range(coils):
-        rows = pl.ds(c * HALF, HALF)
         for slot in range(3):
             s_re = load(c, slot if slot < 2 else 4)
             s_im = load(c, slot + 2 if slot < 2 else 5)
             d_re, d_im = image_ref[0, slot], image_ref[1, slot]
-            for part, value in enumerate((s_re * d_re - s_im * d_im, s_re * d_im + s_im * d_re)):
-                base = part * 2 * LANES
-                for term, half in enumerate(halves(value)):
-                    if slot < 2:
-                        line_ref[term, slot, rows, base : base + LANES] = half
-                    else:
-                        for row in range(2):
-                            line_ref[term, row, rows, base + LANES : base + 2 * LANES] = half
+            x_re = s_re * d_re - s_im * d_im
+            x_im = s_re * d_im + s_im * d_re
+            if slot < 2:
+                store_line(slot, c, 0, x_re)
+                store_line(slot, c, 1, x_im)
+            else:
+                store_line(0, c, 2, join_low(x_re, x_im))
+                store_line(1, c, 2, join_high(x_re, x_im))
     for row in range(2):
-        spectra = dot3(line_ref[0, row], line_ref[1, row], fwd_y_ref[0, row], fwd_y_ref[1, row])
+        spectra = dot3(line_ref[0, row], line_ref[1, row], fwd_y_ref[0], fwd_y_ref[1])
         for term, half in enumerate(halves(spectra)):
             for c in range(coils):
                 mid_ref[term, c, row * HALF : (row + 1) * HALF, :] = half[c * HALF : (c + 1) * HALF]
-    weight_low = weight_ref[:, :LANES].astype(jnp.float32)
-    weight_high = weight_ref[:, LANES:].astype(jnp.float32)
+    weight_low = weight_ref[:LANES].astype(jnp.float32).T
+    weight_high = weight_ref[LANES:].astype(jnp.float32).T
     weight_mix = jnp.concatenate([weight_high, weight_high], axis=1)
     sign = jnp.where(lane_index(LANES) < HALF, 1.0, -1.0).astype(jnp.float32)
     for c in range(coils):
@@ -195,26 +202,22 @@
             p[:, LANES : 2 * LANES] + q[:, :LANES],
             p[:, 2 * LANES :] - turned,
         )
-        for group, value in enumerate(columns):
-            for term, half in enumerate(halves(value)):
-                for row in range(2):
-                    back_ref[term, row, c * HALF : (c + 1) * HALF, group * LANES : (group + 1) * LANES] = half[
-                        row * HALF : (row + 1) * HALF
-                    ]
+        for column, value in enumerate(columns):
+            for row in range(2):
+                store_line(row, c, column, value[row * HALF : (row + 1) * HALF])
+    lines = [dot3(line_ref[0, row], line_ref[1, row], inv_y_ref[0], inv_y_ref[1]) for row in range(2)]
     for slot in range(3):
-        if slot < 2:
-            value = dot3(back_ref[0, slot], back_ref[1, slot], inv_low_ref[0], inv_low_ref[1])
-        else:
-            value = dot3(back_ref[0, 0], back_ref[1, 0], inv_high_ref[0, 0], inv_high_ref[1, 0]) + dot3(
-                back_ref[0, 1], back_ref[1, 1], inv_high_ref[0, 1], inv_high_ref[1, 1]
-            )
         sum_re = jnp.zeros((HALF, LANES), jnp.float32)
         sum_im = jnp.zeros((HALF, LANES), jnp.float32)
         for c in range(coils):
+            rows = slice(c * HALF, (c + 1) * HALF)
             s_re = load(c, slot if slot < 2 else 4)
             s_im = load(c, slot + 2 if slot < 2 else 5)
-            y_re = value[c * HALF : (c + 1) * HALF, :LANES]
-            y_im = value[c * HALF : (c + 1) * HALF, LANES:]
+            if slot < 2:
+                y_re, y_im = lines[slot][rows, :LANES], lines[slot][rows, LANES : 2 * LANES]
+            else:
+                first, second = lines[0][rows, 2 * LANES :], lines[1][rows, 2 * LANES :]
+                y_re, y_im = join_low(first, second), join_high(first, second)
             sum_re = sum_re + (s_re * y_re + s_im * y_im)
             sum_im = sum_im + (s_re * y_im - s_im * y_re)
         total_ref[0, slot] = sum_re
@@ -226,7 +229,7 @@
     pieces = spread([load(c, MESSAGE_R) for c in range(coils)], own, range(2))
     field_ref[1, 0] = pieces[0][0]
     field_ref[1, 1] = pieces[1][0]
-    field_ref[1, 2] = join_high(pieces[0][1], pieces[1][1])
+    field_ref[1, 2] = join_low(pieces[0][1], pieces[1][1])
 
 
 def finish_kernel(own_ref, other_ref, field_ref, out_ref):
@@ -283,39 +286,45 @@
             next_direction_ref[part, 0, row] = next_residual + beta * direction
 
 
+def normal_scratch(planes):
+    return [
+        pltpu.VMEM((2, 2, planes * HALF, 3 * LANES), jnp.bfloat16),
+        pltpu.VMEM((2, planes, LANES, 3 * LANES), jnp.bfloat16),
+        pltpu.VMEM((2, 3, HALF, LANES), jnp.float32),
+        pltpu.VMEM((2, 3, HALF, LANES), jnp.float32),
+    ]
+
+
 def body(solution, residual, direction, sens_maps, sampling):
     axes = ("coil", "slab")
     devices = lax.axis_size(axes)
     planes = lax.axis_size("coil")
     f32 = jnp.float32
-    params = pltpu.CompilerParams(vmem_limit_bytes=48 * 1024 * 1024)
+    params = pltpu.CompilerParams(vmem_limit_bytes=24 * 1024 * 1024)
+    hbm = pl.BlockSpec(memory_space=pltpu.HBM)
+    whole = pl.BlockSpec(memory_space=pltpu.VMEM)
     packed = pl.pallas_call(
         pack_kernel,
+        in_specs=[hbm] * 3,
         out_shape=jax.ShapeDtypeStruct((devices * ROWS, LANES), f32),
+        scratch_shapes=[pltpu.VMEM(a.shape, f32) for a in (sens_maps, direction, residual)]
+        + [pltpu.SemaphoreType.DMA((2, 2)), pltpu.SemaphoreType.DMA((2,))],
         compiler_params=params,
         name="pack",
     )(sens_maps, direction, residual)
+    core = (lax.axis_index("slab") % 2).astype(jnp.int32).reshape(1)
+    packed, core = lax.optimization_barrier((packed, core))
     moved = lax.all_to_all(packed.reshape(devices, ROWS, LANES), axes, 0, 0, tiled=True)
     tables = [jnp.asarray(t) for t in make_tables(sampling.shape[1], sampling.shape[2])]
-    core = (lax.axis_index("slab") % 2).astype(jnp.int32).reshape(1)
-    lines = planes * HALF
-    bf16 = jnp.bfloat16
-    whole = pl.BlockSpec(memory_space=pltpu.VMEM)
     part = jax.ShapeDtypeStruct((3, HALF, LANES), f32)
     own, send, field = pl.pallas_call(
         normal_kernel,
-        in_specs=[pl.BlockSpec(memory_space=pltpu.SMEM)] + [whole] * 7,
+        in_specs=[pl.BlockSpec(memory_space=pltpu.SMEM)] + [whole] * (2 + len(tables)),
         out_shape=(part, part, jax.ShapeDtypeStruct((2, 3, HALF, LANES), f32)),
-        scratch_shapes=[
-            pltpu.VMEM((2, 2, lines, 4 * LANES), bf16),
-            pltpu.VMEM((2, planes, LANES, 3 * LANES), bf16),
-            pltpu.VMEM((2, 2, lines, 3 * LANES), bf16),
-            pltpu.VMEM((2, 3, HALF, LANES), f32),
-            pltpu.VMEM((2, 3, HALF, LANES), f32),
-        ],
+        scratch_shapes=normal_scratch(planes),
         compiler_params=params,
         name="normal",
-    )(core, moved.reshape(devices * ROWS, LANES), sampling[0], *tables)
+    )(core, moved.reshape(devices * ROWS, LANES), sampling[0].T, *tables)
     swap = [(i, i ^ 1) for i in range(lax.axis_size("slab"))]
     other = lax.ppermute(send, "slab", swap)
     result = pl.pallas_call(

time: 126 us -> 122 us (0.968)
  blocking collectives: 26.7 us -> 103 us
  waiting for transfers between devices: 53.9 us -> 0.92 us
  starting transfers between devices: 25.7 us -> 3.54 us
  local copies, waits for them, and re-layouts: 7.84 us -> 3.24 us
    all_to_all x0 -> x1, blocking collectives: none -> 76 us  [body(): lax.all_to_all(packed.reshape(devices, ROWS, LANES), axes, 0, 0, tiled=True)]
    all_to_all x1 -> x0, waiting for transfers between devices: 53 us -> none  [body(): lax.all_to_all(packed.reshape(devices, ROWS, LANES), axes, 0, 0, tiled=True)]
    all_to_all x1 -> x0, starting transfers between devices: 22.2 us -> none  [body(): lax.all_to_all(packed.reshape(devices, ROWS, LANES), axes, 0, 0, tiled=True)]
    unnamed x25 -> x22, local copies, waits for them, and re-layouts: 7.84 us -> 3.24 us
    pallas_call x1, Pallas kernels: 8.29 us -> 6.8 us  [body(): pl.pallas_call(normal_kernel, in_specs=[pl.BlockSpec(memory_space=pltpu.S...]
  transfers between devices with their start and end apart: 2 -> 1, of which waited for: 2 -> 1; matrix products, arithmetic and copies ran while one was open for 1% -> 0% of each run, Pallas kernels for 0% -> 0%
where the time goes in v2:
time: 122 us; the launch traced here: 121 us
  blocking collectives  103 us (84%)
  Pallas kernels  10.3 us (8%)
  starting transfers between devices  3.54 us (3%)
  local copies, waits for them, and re-layouts  3.24 us (3%)
    all_to_all x1, blocking collectives, body(): lax.all_to_all(packed.reshape(devices, ROWS, LANES), axes, 0, 0, tiled=True)  76 us
    all_to_all x1, blocking collectives, body(): lax.all_to_all(result.reshape(devices, 1, LANES), axes, 0, 0, tiled=True)  26.7 us
    pallas_call x1, Pallas kernels, body(): pl.pallas_call(normal_kernel, in_specs=[pl.BlockSpec(memory_space=pltpu.S...  6.8 us
    ppermute x1, starting transfers between devices, body(): other = lax.ppermute(send, 'slab', swap)  3.54 us
    unnamed x22, local copies, waits for them, and re-layouts  3.24 us
  transfers between devices with their start and end apart: 1, of which 1 were waited for; matrix products, arithmetic and copies ran while one was open for 0% of the time, Pallas kernels for 0%

profile of v2, /device:TPU:1, one launch (start us, length us, event | category | flops | bytes accessed | tf_op | source)
XLA Modules:
  0.0 121.4 jit_solution(1127299420765348884)
XLA Ops:
  0.6 0.0 copy-start
  0.7 1.4 %copy-done = f32[2,2,2,192,256]{4,3,2,1,0:T(8,128)S(1)} copy-done((f32[2,2,2,192,256]{4,3,2,1,0:T(8,128)S(1)}, f32[2,2,2,192,256]{4,3,2,1,0:T(8,128)}, u32[]{:S(2)}) %copy-start) | copy-done | bytes 1572888
  2.0 0.0 copy-start.3
  2.1 0.9 copy-done.3
  2.9 0.0 copy-start.5
  2.9 0.9 copy-done.5
  3.8 2.4 %pack.1 = f32[4096,128]{1,0:T(8,128)S(1)} custom-call(f32[2,2,2,192,256]{4,3,2,1,0:T(8,128)S(1)} %copy-done, f32[2,1,2,24,256]{4,3,2,1,0:T(8,128)S(1)} %copy-done.3, f32[2,1,2,24,256]{4,3,2,1,0:T(8,128)S(1)} %copy-done.5), custom_call_target="tpu_custom_call" | custom-call | tf_op jit(solution)/shard_map/pack/pallas_call | solution.py:306
  6.2 0.0 copy-start.1
  6.2 0.0 copy-start.2
  6.2 0.0 copy-start.7
  6.2 0.0 copy-start.8
  6.3 0.0 copy-start.10
  6.3 76.0 %all_to_all.10 = f32[512,8,128]{2,1,0:T(8,128)S(1)} all-to-all(f32[512,8,128]{2,1,0:T(8,128)S(1)} %bitcast.11), channel_id=1, replica_groups=mesh['coil'=8,'slab'=64] {'coil','slab'}, dimensions={0} | all-to-all | bytes 4194304 | tf_op jit(solution)/shard_map/all_to_all | solution.py:317
  82.2 0.0 copy-done.1
  82.2 0.0 copy-done.2
  82.2 0.0 copy-done.7
  82.2 0.0 copy-done.8
  82.2 0.0 copy-done.10
  82.3 0.0 copy-start.4
  82.3 0.0 copy-start.6
  82.3 0.0 copy-start.9
  82.3 6.8 %normal.1 = (f32[3,64,128]{2,1,0:T(8,128)S(1)}, f32[3,64,128]{2,1,0:T(8,128)S(1)}, f32[2,3,64,128]{3,2,1,0:T(8,128)S(1)}) custom-call(s32[1]{0:T(128)} %bitcast.core_ref, f32[4096,128]{1,0:T(8,128)S(1)} %bitcast.10, s32[192,128]{1,0:T(8,128)S(1)} %bitcast.14, bf16[2,384,384]{2,1,0:T(8,128)(2,1)S(1)} %copy-done.2, bf16[2,384,384]{2,1,0:T(8,128)(2,1)S(1)} %copy-done.1, ...), custom_call_target="tpu_custom_call" | custom-call | tf_op jit(solution)/shard_map/normal/pallas_call | solution.py:320
  89.1 3.5 %collective-permute-start = (f32[3,64,128]{2,1,0:T(8,128)S(1)}, f32[3,64,128]{2,1,0:T(8,128)S(1)}, u32[]{:S(2)}, u32[]{:S(2)}) collective-permute-start(f32[3,64,128]{2,1,0:T(8,128)S(1)} %get-tuple-element.11), channel_id=1, source_target_pairs={{0,1},{1,0},{2,3},{3,2},{4,5},{5,4},{6,7},{7,6},{8,9},{9,8},{10,11... | collective-permute-start | bytes 294920 | tf_op jit(solution)/shard_map/ppermute | solution.py:329
  92.6 0.9 collective-permute-done.other_ref
  93.6 0.3 finish.1
  93.8 26.7 %all_to_all.11 = f32[512,1,128]{2,1,0:T(1,128)S(1)} all-to-all(f32[512,1,128]{2,1,0:T(1,128)S(1)} %bitcast.13), channel_id=1, replica_groups=mesh['coil'=8,'slab'=64] {'coil','slab'}, dimensions={0} | all-to-all | bytes 524288 | tf_op jit(solution)/shard_map/all_to_all | solution.py:336
  120.5 0.0 copy-done.4
  120.5 0.0 copy-done.6
  120.5 0.0 copy-done.9
  120.5 0.9 update.1
Async XLA Ops:
  0.6 1.4 %copy-start = (f32[2,2,2,192,256]{4,3,2,1,0:T(8,128)S(1)}, f32[2,2,2,192,256]{4,3,2,1,0:T(8,128)}, u32[]{:S(2)}) copy-start(f32[2,2,2,192,256]{4,3,2,1,0:T(8,128)} %maps_hbm.1) | copy-start | bytes 4718596
  2.0 0.9 copy-start.3
  2.9 0.9 copy-start.5
  6.2 76.0 %copy-start.1 = (bf16[2,384,384]{2,1,0:T(8,128)(2,1)S(1)}, bf16[2,384,384]{2,1,0:T(8,128)(2,1)}, u32[]{:S(2)}) copy-start(bf16[2,384,384]{2,1,0:T(8,128)(2,1)} %constant.26.clone.inv_y_ref) | copy-start | bytes 1769476
  6.2 76.0 %copy-start.2 = (bf16[2,384,384]{2,1,0:T(8,128)(2,1)S(1)}, bf16[2,384,384]{2,1,0:T(8,128)(2,1)}, u32[]{:S(2)}) copy-start(bf16[2,384,384]{2,1,0:T(8,128)(2,1)} %constant.25.clone.fwd_y_ref) | copy-start | bytes 1769476
  6.2 76.0 %copy-start.7 = (bf16[2,256,128]{2,1,0:T(8,128)(2,1)S(1)}, bf16[2,256,128]{2,1,0:T(8,128)(2,1)}, u32[]{:S(2)}) copy-start(bf16[2,256,128]{2,1,0:T(8,128)(2,1)} %constant.28.clone.inv_x_ref) | copy-start | bytes 393220
  6.2 76.0 %copy-start.8 = (bf16[2,256,128]{2,1,0:T(8,128)(2,1)S(1)}, bf16[2,256,128]{2,1,0:T(8,128)(2,1)}, u32[]{:S(2)}) copy-start(bf16[2,256,128]{2,1,0:T(8,128)(2,1)} %constant.27.clone.fwd_x_ref) | copy-start | bytes 393220
  6.3 76.0 %copy-start.10 = (s32[1,128,192]{1,2,0:T(8,128)S(1)}, s32[1,128,192]{1,2,0:T(8,128)}, u32[]{:S(2)}) copy-start(s32[1,128,192]{1,2,0:T(8,128)} %param.13) | copy-start | bytes 294916
  82.3 38.3 %copy-start.4 = (f32[2,1,2,24,256]{4,3,2,1,0:T(8,128)S(1)}, f32[2,1,2,24,256]{4,3,2,1,0:T(8,128)}, u32[]{:S(2)}) copy-start(f32[2,1,2,24,256]{4,3,2,1,0:T(8,128)} %direction_ref.1) | copy-start | bytes 294916
  82.3 38.2 %copy-start.6 = (f32[2,1,2,24,256]{4,3,2,1,0:T(8,128)S(1)}, f32[2,1,2,24,256]{4,3,2,1,0:T(8,128)}, u32[]{:S(2)}) copy-start(f32[2,1,2,24,256]{4,3,2,1,0:T(8,128)} %residual_ref.1) | copy-start | bytes 294916
  82.3 38.2 %copy-start.9 = (f32[2,1,2,24,256]{4,3,2,1,0:T(8,128)S(1)}, f32[2,1,2,24,256]{4,3,2,1,0:T(8,128)}, u32[]{:S(2)}) copy-start(f32[2,1,2,24,256]{4,3,2,1,0:T(8,128)} %solution_ref.1) | copy-start | bytes 294916
  89.1 4.5 %collective-permute-start = (f32[3,64,128]{2,1,0:T(8,128)S(1)}, f32[3,64,128]{2,1,0:T(8,128)S(1)}, u32[]{:S(2)}, u32[]{:S(2)}) collective-permute-start(f32[3,64,128]{2,1,0:T(8,128)S(1)} %get-tuple-element.11), channel_id=1, source_target_pairs={{0,1},{1,0},{2,3},{3,2},{4,5},{5,4},{6,7},{7,6},{8,9},{9,8},{10,11... | collective-permute-start | bytes 294920 | tf_op jit(solution)/shard_map/ppermute | solution.py:329

commit v3 on v2

--- a/solution.py
+++ b/solution.py
@@ -301,7 +301,7 @@
     planes = lax.axis_size("coil")
     f32 = jnp.float32
     params = pltpu.CompilerParams(vmem_limit_bytes=24 * 1024 * 1024)
-    hbm = pl.BlockSpec(memory_space=pltpu.HBM)
+    hbm = pl.BlockSpec(memory_space=pl.ANY)
     whole = pl.BlockSpec(memory_space=pltpu.VMEM)
     packed = pl.pallas_call(
         pack_kernel,
@@ -311,7 +311,7 @@
         + [pltpu.SemaphoreType.DMA((2, 2)), pltpu.SemaphoreType.DMA((2,))],
         compiler_params=params,
         name="pack",
-    )(sens_maps, direction, residual)
+    )(*(pltpu.with_memory_space_constraint(a, pltpu.HBM) for a in (sens_maps, direction, residual)))
     core = (lax.axis_index("slab") % 2).astype(jnp.int32).reshape(1)
     packed, core = lax.optimization_barrier((packed, core))
     moved = lax.all_to_all(packed.reshape(devices, ROWS, LANES), axes, 0, 0, tiled=True)

time: 122 us -> 119 us (0.975)
  local copies, waits for them, and re-layouts: 3.24 us -> 0.05 us
    unnamed x22 -> x16, local copies, waits for them, and re-layouts: 3.24 us -> 0.05 us
where the time goes in v3:
time: 119 us
  blocking collectives  103 us (87%)
  Pallas kernels  10.6 us (9%)
  starting transfers between devices  3.54 us (3%)
    all_to_all x1, blocking collectives, body(): lax.all_to_all(packed.reshape(devices, ROWS, LANES), axes, 0, 0, tiled=True)  76 us
    all_to_all x1, blocking collectives, body(): lax.all_to_all(result.reshape(devices, 1, LANES), axes, 0, 0, tiled=True)  26.7 us
    pallas_call x1, Pallas kernels, body(): pl.pallas_call(normal_kernel, in_specs=[pl.BlockSpec(memory_space=pltpu.S...  6.8 us
    ppermute x1, starting transfers between devices, body(): other = lax.ppermute(send, 'slab', swap)  3.54 us
    pallas_call x1, Pallas kernels, body(): pl.pallas_call(pack_kernel, in_specs=[hbm] * 3, out_shape=jax.ShapeDtypeS...  2.67 us
  transfers between devices with their start and end apart: 1, of which 1 were waited for; matrix products, arithmetic and copies ran while one was open for 0% of the time, Pallas kernels for 0%

profile of v3, /device:TPU:1, one launch (start us, length us, event | category | flops | bytes accessed | tf_op | source)
XLA Modules:
  0.0 118.5 jit_solution(3557688692801351395)
XLA Ops:
  0.6 2.7 %pack.1 = f32[4096,128]{1,0:T(8,128)S(1)} custom-call(f32[2,2,2,192,256]{4,3,2,1,0:T(8,128)} %maps_hbm.1, f32[2,1,2,24,256]{4,3,2,1,0:T(8,128)} %direction_ref.1, f32[2,1,2,24,256]{4,3,2,1,0:T(8,128)} %residual_ref.1), custom_call_target="tpu_custom_call" | custom-call | tf_op jit(solution)/shard_map/pack/pallas_call | solution.py:306
  3.3 0.0 copy-start
  3.3 0.0 copy-start.1
  3.3 0.0 copy-start.4
  3.4 0.0 copy-start.5
  3.4 0.0 copy-start.7
  3.4 76.0 %all_to_all.10 = f32[512,8,128]{2,1,0:T(8,128)S(1)} all-to-all(f32[512,8,128]{2,1,0:T(8,128)S(1)} %bitcast.11), channel_id=1, replica_groups=mesh['coil'=8,'slab'=64] {'coil','slab'}, dimensions={0} | all-to-all | bytes 4194304 | tf_op jit(solution)/shard_map/all_to_all | solution.py:317
  79.3 0.0 copy-done
  79.3 0.0 copy-done.1
  79.3 0.0 copy-done.4
  79.4 0.0 copy-done.5
  79.4 0.0 copy-done.7
  79.4 0.0 copy-start.2
  79.4 0.0 copy-start.3
  79.4 0.0 copy-start.6
  79.4 6.8 %normal.1 = (f32[3,64,128]{2,1,0:T(8,128)S(1)}, f32[3,64,128]{2,1,0:T(8,128)S(1)}, f32[2,3,64,128]{3,2,1,0:T(8,128)S(1)}) custom-call(s32[1]{0:T(128)} %bitcast.core_ref, f32[4096,128]{1,0:T(8,128)S(1)} %bitcast.10, s32[192,128]{1,0:T(8,128)S(1)} %bitcast.14, bf16[2,384,384]{2,1,0:T(8,128)(2,1)S(1)} %copy-done.1, bf16[2,384,384]{2,1,0:T(8,128)(2,1)S(1)} %copy-done, ...), custom_call_target="tpu_custom_call" | custom-call | tf_op jit(solution)/shard_map/normal/pallas_call | solution.py:320
  86.2 3.5 %collective-permute-start = (f32[3,64,128]{2,1,0:T(8,128)S(1)}, f32[3,64,128]{2,1,0:T(8,128)S(1)}, u32[]{:S(2)}, u32[]{:S(2)}) collective-permute-start(f32[3,64,128]{2,1,0:T(8,128)S(1)} %get-tuple-element.11), channel_id=1, source_target_pairs={{0,1},{1,0},{2,3},{3,2},{4,5},{5,4},{6,7},{7,6},{8,9},{9,8},{10,11... | collective-permute-start | bytes 294920 | tf_op jit(solution)/shard_map/ppermute | solution.py:329
  89.8 0.9 collective-permute-done.other_ref
  90.7 0.3 finish.1
  90.9 26.7 %all_to_all.11 = f32[512,1,128]{2,1,0:T(1,128)S(1)} all-to-all(f32[512,1,128]{2,1,0:T(1,128)S(1)} %bitcast.13), channel_id=1, replica_groups=mesh['coil'=8,'slab'=64] {'coil','slab'}, dimensions={0} | all-to-all | bytes 524288 | tf_op jit(solution)/shard_map/all_to_all | solution.py:336
  117.6 0.0 copy-done.2
  117.6 0.0 copy-done.3
  117.6 0.0 copy-done.6
  117.6 0.9 update.1
Async XLA Ops:
  3.3 76.0 %copy-start = (bf16[2,384,384]{2,1,0:T(8,128)(2,1)S(1)}, bf16[2,384,384]{2,1,0:T(8,128)(2,1)}, u32[]{:S(2)}) copy-start(bf16[2,384,384]{2,1,0:T(8,128)(2,1)} %constant.26.clone.inv_y_ref) | copy-start | bytes 1769476
  3.3 76.0 %copy-start.1 = (bf16[2,384,384]{2,1,0:T(8,128)(2,1)S(1)}, bf16[2,384,384]{2,1,0:T(8,128)(2,1)}, u32[]{:S(2)}) copy-start(bf16[2,384,384]{2,1,0:T(8,128)(2,1)} %constant.25.clone.fwd_y_ref) | copy-start | bytes 1769476
  3.3 76.0 %copy-start.4 = (bf16[2,256,128]{2,1,0:T(8,128)(2,1)S(1)}, bf16[2,256,128]{2,1,0:T(8,128)(2,1)}, u32[]{:S(2)}) copy-start(bf16[2,256,128]{2,1,0:T(8,128)(2,1)} %constant.28.clone.inv_x_ref) | copy-start | bytes 393220
  3.4 76.0 %copy-start.5 = (bf16[2,256,128]{2,1,0:T(8,128)(2,1)S(1)}, bf16[2,256,128]{2,1,0:T(8,128)(2,1)}, u32[]{:S(2)}) copy-start(bf16[2,256,128]{2,1,0:T(8,128)(2,1)} %constant.27.clone.fwd_x_ref) | copy-start | bytes 393220
  3.4 76.0 %copy-start.7 = (s32[1,128,192]{1,2,0:T(8,128)S(1)}, s32[1,128,192]{1,2,0:T(8,128)}, u32[]{:S(2)}) copy-start(s32[1,128,192]{1,2,0:T(8,128)} %param.13) | copy-start | bytes 294916
  79.4 38.3 %copy-start.2 = (f32[2,1,2,24,256]{4,3,2,1,0:T(8,128)S(1)}, f32[2,1,2,24,256]{4,3,2,1,0:T(8,128)}, u32[]{:S(2)}) copy-start(f32[2,1,2,24,256]{4,3,2,1,0:T(8,128)} %direction_ref.1) | copy-start | bytes 294916
  79.4 38.2 %copy-start.3 = (f32[2,1,2,24,256]{4,3,2,1,0:T(8,128)S(1)}, f32[2,1,2,24,256]{4,3,2,1,0:T(8,128)}, u32[]{:S(2)}) copy-start(f32[2,1,2,24,256]{4,3,2,1,0:T(8,128)} %residual_ref.1) | copy-start | bytes 294916
  79.4 38.2 %copy-start.6 = (f32[2,1,2,24,256]{4,3,2,1,0:T(8,128)S(1)}, f32[2,1,2,24,256]{4,3,2,1,0:T(8,128)}, u32[]{:S(2)}) copy-start(f32[2,1,2,24,256]{4,3,2,1,0:T(8,128)} %solution_ref.1) | copy-start | bytes 294916
  86.2 4.5 %collective-permute-start = (f32[3,64,128]{2,1,0:T(8,128)S(1)}, f32[3,64,128]{2,1,0:T(8,128)S(1)}, u32[]{:S(2)}, u32[]{:S(2)}) collective-permute-start(f32[3,64,128]{2,1,0:T(8,128)S(1)} %get-tuple-element.11), channel_id=1, source_target_pairs={{0,1},{1,0},{2,3},{3,2},{4,5},{5,4},{6,7},{7,6},{8,9},{9,8},{10,11... | collective-permute-start | bytes 294920 | tf_op jit(solution)/shard_map/ppermute | solution.py:329

commit v4 on v3

--- a/solution.py
+++ b/solution.py
@@ -12,9 +12,8 @@
 damping_weight = 0.5
 
 LANES = 128
-ROWS = 8
-MESSAGE_D = 6
-MESSAGE_R = 7
+ROWS = 7
+MESSAGE_IMAGE = 6
 HALF = 64
 SUMS_AT = 48
 
@@ -64,13 +63,10 @@
     for copy in images:
         copy.wait()
     own = direction_ref.shape[3]
-    pieces = [direction_ref[part, 0, row] for part in range(2) for row in range(2)]
     filler = jnp.zeros((LANES - 4 * own, cells), jnp.float32)
-    field = jnp.concatenate(pieces + [filler], axis=0)
     for core in range(2):
-        put(core, MESSAGE_D, field)
-        filler = jnp.zeros((LANES - 2 * own, cells), jnp.float32)
-        put(core, MESSAGE_R, jnp.concatenate([residual_ref[core, 0, 0], residual_ref[core, 0, 1], filler], axis=0))
+        pieces = [image_ref[core, 0, row] for image_ref in (direction_ref, residual_ref) for row in range(2)]
+        put(core, MESSAGE_IMAGE, jnp.concatenate(pieces + [filler], axis=0))
     for core in range(2):
         for part in range(2):
             copies[core * 2 + part].wait()
@@ -126,9 +122,26 @@
     return dot(left_high, right_high) + (dot(left_high, right_low) + dot(left_low, right_high))
 
 
+def load_rows(recv_ref, c, slot):
+    return recv_ref[pl.ds(c * HALF * ROWS + slot, HALF, stride=ROWS), :]
+
+
+def image_kernel(recv_ref, direction_ref, residual_ref):
+    coils = recv_ref.shape[0] // (ROWS * HALF)
+    own = 2 * 96 // coils
+    pieces = spread([load_rows(recv_ref, c, MESSAGE_IMAGE) for c in range(coils)], own, range(4))
+    for index, image_ref in enumerate((direction_ref, residual_ref)):
+        (low0, high0), (low1, high1) = pieces[2 * index], pieces[2 * index + 1]
+        image_ref[0] = low0
+        image_ref[1] = low1
+        image_ref[2] = join_low(high0, high1)
+
+
 def normal_kernel(
     core_ref,
     recv_ref,
+    own_image_ref,
+    other_image_ref,
     weight_ref,
     fwd_y_ref,
     inv_y_ref,
@@ -136,24 +149,19 @@
     inv_x_ref,
     own_ref,
     send_ref,
-    field_ref,
     line_ref,
     mid_ref,
     total_ref,
     image_ref,
 ):
     coils = recv_ref.shape[0] // (ROWS * HALF)
-    own = 2 * 96 // coils
+    core = core_ref[0]
 
     def load(c, slot):
-        return recv_ref[pl.ds(c * HALF * ROWS + slot, HALF, stride=ROWS), :]
-
-    pieces = spread([load(c, MESSAGE_D) for c in range(coils)], own, range(4))
-    for part in range(2):
-        (low0, high0), (low1, high1) = pieces[2 * part], pieces[2 * part + 1]
-        image_ref[part, 0] = low0
-        image_ref[part, 1] = low1
-        image_ref[part, 2] = join_low(high0, high1)
+        return load_rows(recv_ref, c, slot)
+
+    image_ref[core] = own_image_ref[...]
+    image_ref[1 - core] = other_image_ref[...]
 
     def store_line(row, c, column, value):
         for term, half in enumerate(halves(value)):
@@ -222,19 +230,13 @@
             sum_im = sum_im + (s_re * y_im - s_im * y_re)
         total_ref[0, slot] = sum_re
         total_ref[1, slot] = sum_im
-    core = core_ref[0]
     own_ref[...] = total_ref[core]
     send_ref[...] = total_ref[1 - core]
-    field_ref[0] = image_ref[core]
-    pieces = spread([load(c, MESSAGE_R) for c in range(coils)], own, range(2))
-    field_ref[1, 0] = pieces[0][0]
-    field_ref[1, 1] = pieces[1][0]
-    field_ref[1, 2] = join_low(pieces[0][1], pieces[1][1])
-
-
-def finish_kernel(own_ref, other_ref, field_ref, out_ref):
-    direction = field_ref[0]
-    residual = field_ref[1]
+
+
+def finish_kernel(own_ref, other_ref, direction_ref, residual_ref, out_ref):
+    direction = direction_ref[...]
+    residual = residual_ref[...]
     image_ap = own_ref[...] + other_ref[...] + damping_weight * direction
     lane = lane_index(HALF)
     coils = out_ref.shape[0] // HALF
@@ -314,25 +316,30 @@
     )(*(pltpu.with_memory_space_constraint(a, pltpu.HBM) for a in (sens_maps, direction, residual)))
     core = (lax.axis_index("slab") % 2).astype(jnp.int32).reshape(1)
     packed, core = lax.optimization_barrier((packed, core))
-    moved = lax.all_to_all(packed.reshape(devices, ROWS, LANES), axes, 0, 0, tiled=True)
+    moved = lax.all_to_all(packed.reshape(devices * ROWS, 1, LANES), axes, 0, 0, tiled=True)
+    moved = moved.reshape(devices * ROWS, LANES)
     tables = [jnp.asarray(t) for t in make_tables(sampling.shape[1], sampling.shape[2])]
+    swap = [(i, i ^ 1) for i in range(lax.axis_size("slab"))]
     part = jax.ShapeDtypeStruct((3, HALF, LANES), f32)
-    own, send, field = pl.pallas_call(
+    image, residual_image = pl.pallas_call(
+        image_kernel, out_shape=(part, part), compiler_params=params, name="image"
+    )(moved)
+    other_image = lax.ppermute(image, "slab", swap)
+    own, send = pl.pallas_call(
         normal_kernel,
-        in_specs=[pl.BlockSpec(memory_space=pltpu.SMEM)] + [whole] * (2 + len(tables)),
-        out_shape=(part, part, jax.ShapeDtypeStruct((2, 3, HALF, LANES), f32)),
+        in_specs=[pl.BlockSpec(memory_space=pltpu.SMEM)] + [whole] * (4 + len(tables)),
+        out_shape=(part, part),
         scratch_shapes=normal_scratch(planes),
         compiler_params=params,
         name="normal",
-    )(core, moved.reshape(devices * ROWS, LANES), sampling[0].T, *tables)
-    swap = [(i, i ^ 1) for i in range(lax.axis_size("slab"))]
+    )(core, moved, image, other_image, sampling[0].T, *tables)
     other = lax.ppermute(send, "slab", swap)
     result = pl.pallas_call(
         finish_kernel,
         out_shape=jax.ShapeDtypeStruct((devices, LANES), f32),
         compiler_params=params,
         name="finish",
-    )(own, other, field)
+    )(own, other, image, residual_image)
     home = lax.all_to_all(result.reshape(devices, 1, LANES), axes, 0, 0, tiled=True).reshape(devices, LANES)
     out = jax.ShapeDtypeStruct(direction.shape, f32)
     return tuple(

time: 119 us -> 116 us (0.975)
  blocking collectives: 103 us -> 97 us
  starting transfers between devices: 3.54 us -> 6.01 us
    all_to_all x1, blocking collectives: 76 us -> 70.4 us  [body(): lax.all_to_all(packed.reshape(devices * ROWS, 1, LANES), axes, 0, 0, tile...]
    ppermute x0 -> x1, starting transfers between devices: none -> 3.74 us  [body(): other_image = lax.ppermute(image, 'slab', swap)]
    ppermute x1, starting transfers between devices: 3.54 us -> 2.27 us  [body(): other = lax.ppermute(send, 'slab', swap)]
  transfers between devices with their start and end apart: 1 -> 2, of which waited for: 1 -> 2; matrix products, arithmetic and copies ran while one was open for 0% -> 0% of each run, Pallas kernels for 0% -> 0%
where the time goes in v4:
time: 116 us
  blocking collectives  97 us (84%)
  Pallas kernels  9.96 us (9%)
  starting transfers between devices  6.01 us (5%)
  waiting for transfers between devices  1.84 us (2%)
    all_to_all x1, blocking collectives, body(): lax.all_to_all(packed.reshape(devices * ROWS, 1, LANES), axes, 0, 0, tile...  70.4 us
    all_to_all x1, blocking collectives, body(): lax.all_to_all(result.reshape(devices, 1, LANES), axes, 0, 0, tiled=True)  26.7 us
    pallas_call x1, Pallas kernels, body(): pl.pallas_call(normal_kernel, in_specs=[pl.BlockSpec(memory_space=pltpu.S...  6.33 us
    ppermute x1, starting transfers between devices, body(): other_image = lax.ppermute(image, 'slab', swap)  3.74 us
  transfers between devices with their start and end apart: 2, of which 2 were waited for; matrix products, arithmetic and copies ran while one was open for 0% of the time, Pallas kernels for 0%

profile of v4, /device:TPU:1, one launch (start us, length us, event | category | flops | bytes accessed | tf_op | source)
XLA Modules:
  0.0 115.6 jit_solution(177005710891006994)
XLA Ops:
  0.6 2.1 %pack.1 = f32[3584,128]{1,0:T(8,128)S(1)} custom-call(f32[2,2,2,192,256]{4,3,2,1,0:T(8,128)} %maps_hbm.1, f32[2,1,2,24,256]{4,3,2,1,0:T(8,128)} %direction_ref.1, f32[2,1,2,24,256]{4,3,2,1,0:T(8,128)} %residual_ref.1), custom_call_target="tpu_custom_call" | custom-call | tf_op jit(solution)/shard_map/pack/pallas_call | solution.py:308
  2.8 70.4 %all_to_all.10 = f32[3584,1,128]{2,1,0:T(1,128)S(1)} all-to-all(f32[3584,1,128]{2,1,0:T(1,128)S(1)} %bitcast.14), channel_id=1, replica_groups=mesh['coil'=8,'slab'=64] {'coil','slab'}, dimensions={0} | all-to-all | bytes 3670016 | tf_op jit(solution)/shard_map/all_to_all | solution.py:319
  73.2 0.0 copy-start
  73.2 0.0 copy-start.1
  73.2 0.0 copy-start.4
  73.2 0.0 copy-start.5
  73.2 0.0 copy-start.7
  73.2 0.3 image.1
  73.5 3.7 %collective-permute-start = (f32[3,64,128]{2,1,0:T(8,128)S(1)}, f32[3,64,128]{2,1,0:T(8,128)S(1)}, u32[]{:S(2)}, u32[]{:S(2)}) collective-permute-start(f32[3,64,128]{2,1,0:T(8,128)S(1)} %get-tuple-element.11.own_image_ref.direction_ref), channel_id=1, source_target_pairs={{0,1},{1,0},{2,3},{3,2},{4,5},{5,4},{6,7},{7,6},{8,9},{9,8},{10,11... | collective-permute-start | bytes 294920 | tf_op jit(solution)/shard_map/ppermute | solution.py:327
  77.3 0.9 collective-permute-done.other_image_ref
  78.2 0.0 copy-done
  78.2 0.0 copy-done.1
  78.2 0.0 copy-done.4
  78.2 0.0 copy-done.5
  78.2 0.0 copy-done.7
  78.2 0.0 copy-start.2
  78.2 0.0 copy-start.3
  78.2 0.0 copy-start.6
  78.3 6.3 %normal.1 = (f32[3,64,128]{2,1,0:T(8,128)S(1)}, f32[3,64,128]{2,1,0:T(8,128)S(1)}) custom-call(s32[1]{0:T(128)} %bitcast.core_ref, f32[3584,128]{1,0:T(8,128)S(1)} %bitcast.13, f32[3,64,128]{2,1,0:T(8,128)S(1)} %get-tuple-element.11.own_image_ref.direction_ref, f32[3,64,128]{2,1,0:T(8,128)S(1)} %collective-permute-done.other_image_ref, ...), custom_call_target="tpu_custom_call" | custom-call | tf_op jit(solution)/shard_map/normal/pallas_call | solution.py:328
  84.6 2.3 %collective-permute-start.1 = (f32[3,64,128]{2,1,0:T(8,128)S(1)}, f32[3,64,128]{2,1,0:T(8,128)S(1)}, u32[]{:S(2)}, u32[]{:S(2)}) collective-permute-start(f32[3,64,128]{2,1,0:T(8,128)S(1)} %get-tuple-element.13), channel_id=1, source_target_pairs={{0,1},{1,0},{2,3},{3,2},{4,5},{5,4},{6,7},{7,6},{8,9},{9,8},{10,11... | collective-permute-start | bytes 294920 | tf_op jit(solution)/shard_map/ppermute | solution.py:336
  86.9 0.9 collective-permute-done.1.other_ref
  87.8 0.3 finish.1
  88.0 26.7 %all_to_all.11 = f32[512,1,128]{2,1,0:T(1,128)S(1)} all-to-all(f32[512,1,128]{2,1,0:T(1,128)S(1)} %bitcast.15), channel_id=1, replica_groups=mesh['coil'=8,'slab'=64] {'coil','slab'}, dimensions={0} | all-to-all | bytes 524288 | tf_op jit(solution)/shard_map/all_to_all | solution.py:343
  114.7 0.0 copy-done.2
  114.7 0.0 copy-done.3
  114.7 0.0 copy-done.6
  114.7 0.9 update.1
Async XLA Ops:
  73.2 5.0 %copy-start = (bf16[2,384,384]{2,1,0:T(8,128)(2,1)S(1)}, bf16[2,384,384]{2,1,0:T(8,128)(2,1)}, u32[]{:S(2)}) copy-start(bf16[2,384,384]{2,1,0:T(8,128)(2,1)} %constant.26.clone.inv_y_ref) | copy-start | bytes 1769476
  73.2 5.0 %copy-start.1 = (bf16[2,384,384]{2,1,0:T(8,128)(2,1)S(1)}, bf16[2,384,384]{2,1,0:T(8,128)(2,1)}, u32[]{:S(2)}) copy-start(bf16[2,384,384]{2,1,0:T(8,128)(2,1)} %constant.25.clone.fwd_y_ref) | copy-start | bytes 1769476
  73.2 5.0 %copy-start.4 = (bf16[2,256,128]{2,1,0:T(8,128)(2,1)S(1)}, bf16[2,256,128]{2,1,0:T(8,128)(2,1)}, u32[]{:S(2)}) copy-start(bf16[2,256,128]{2,1,0:T(8,128)(2,1)} %constant.28.clone.inv_x_ref) | copy-start | bytes 393220
  73.2 5.0 %copy-start.5 = (bf16[2,256,128]{2,1,0:T(8,128)(2,1)S(1)}, bf16[2,256,128]{2,1,0:T(8,128)(2,1)}, u32[]{:S(2)}) copy-start(bf16[2,256,128]{2,1,0:T(8,128)(2,1)} %constant.27.clone.fwd_x_ref) | copy-start | bytes 393220
  73.2 5.0 %copy-start.7 = (s32[1,128,192]{1,2,0:T(8,128)S(1)}, s32[1,128,192]{1,2,0:T(8,128)}, u32[]{:S(2)}) copy-start(s32[1,128,192]{1,2,0:T(8,128)} %param.13) | copy-start | bytes 294916
  73.5 4.7 %collective-permute-start = (f32[3,64,128]{2,1,0:T(8,128)S(1)}, f32[3,64,128]{2,1,0:T(8,128)S(1)}, u32[]{:S(2)}, u32[]{:S(2)}) collective-permute-start(f32[3,64,128]{2,1,0:T(8,128)S(1)} %get-tuple-element.11.own_image_ref.direction_ref), channel_id=1, source_target_pairs={{0,1},{1,0},{2,3},{3,2},{4,5},{5,4},{6,7},{7,6},{8,9},{9,8},{10,11... | collective-permute-start | bytes 294920 | tf_op jit(solution)/shard_map/ppermute | solution.py:327
  78.2 36.5 %copy-start.2 = (f32[2,1,2,24,256]{4,3,2,1,0:T(8,128)S(1)}, f32[2,1,2,24,256]{4,3,2,1,0:T(8,128)}, u32[]{:S(2)}) copy-start(f32[2,1,2,24,256]{4,3,2,1,0:T(8,128)} %direction_ref.1) | copy-start | bytes 294916
  78.2 36.5 %copy-start.3 = (f32[2,1,2,24,256]{4,3,2,1,0:T(8,128)S(1)}, f32[2,1,2,24,256]{4,3,2,1,0:T(8,128)}, u32[]{:S(2)}) copy-start(f32[2,1,2,24,256]{4,3,2,1,0:T(8,128)} %residual_ref.1) | copy-start | bytes 294916
  78.2 36.5 %copy-start.6 = (f32[2,1,2,24,256]{4,3,2,1,0:T(8,128)S(1)}, f32[2,1,2,24,256]{4,3,2,1,0:T(8,128)}, u32[]{:S(2)}) copy-start(f32[2,1,2,24,256]{4,3,2,1,0:T(8,128)} %solution_ref.1) | copy-start | bytes 294916
  84.6 3.2 %collective-permute-start.1 = (f32[3,64,128]{2,1,0:T(8,128)S(1)}, f32[3,64,128]{2,1,0:T(8,128)S(1)}, u32[]{:S(2)}, u32[]{:S(2)}) collective-permute-start(f32[3,64,128]{2,1,0:T(8,128)S(1)} %get-tuple-element.13), channel_id=1, source_target_pairs={{0,1},{1,0},{2,3},{3,2},{4,5},{5,4},{6,7},{7,6},{8,9},{9,8},{10,11... | collective-permute-start | bytes 294920 | tf_op jit(solution)/shard_map/ppermute | solution.py:336

commit v5 on v4

--- a/solution.py
+++ b/solution.py
@@ -7,6 +7,7 @@
 from jax import lax
 from jax.experimental import pallas as pl
 from jax.experimental.pallas import tpu as pltpu
+from jax.sharding import Mesh
 from jax.sharding import PartitionSpec as P
 
 damping_weight = 0.5
@@ -15,7 +16,8 @@
 ROWS = 7
 MESSAGE_IMAGE = 6
 HALF = 64
-SUMS_AT = 48
+QUARTER = 32
+SUMS_AT = 96
 
 
 def split_pair(table):
@@ -37,7 +39,7 @@
     re_from_re = np.concatenate([cos_y[:, :LANES], -sin_y[:, :LANES], cos_y[:, LANES:], -sin_y[:, LANES:]], axis=1)
     re_from_im = np.concatenate([sin_y[:, :LANES], cos_y[:, :LANES], sin_y[:, LANES:], cos_y[:, LANES:]], axis=1)
     fwd_y = np.concatenate([re_from_re[:LANES], re_from_im[:LANES], re_from_re[LANES:], re_from_im[LANES:]], axis=0)
-    order = np.concatenate([np.arange(0, size_x, 2), np.arange(1, size_x, 2)])
+    order = np.arange(size_x).reshape(-1, 2, 2).transpose(2, 1, 0).reshape(-1)
     fwd_x = np.concatenate([cos_x[:, order], sin_x[:, order]], axis=0)
     inv_x = np.concatenate([cos_x[order], sin_x[order]], axis=0)
     return [split_pair(t) for t in (fwd_y, fwd_y.T, fwd_x, inv_x)]
@@ -58,7 +60,10 @@
         copy.start()
 
     def put(core, slot, block):
-        out_ref[pl.ds(core * ROWS + slot, cells, stride=2 * ROWS), :] = block.T
+        turned = block.T
+        for plane in range(cells // QUARTER):
+            rows = pl.ds((plane * HALF + core * QUARTER) * ROWS + slot, QUARTER, stride=ROWS)
+            out_ref[rows, :] = turned[plane * QUARTER : (plane + 1) * QUARTER]
 
     for copy in images:
         copy.wait()
@@ -126,15 +131,15 @@
     return recv_ref[pl.ds(c * HALF * ROWS + slot, HALF, stride=ROWS), :]
 
 
-def image_kernel(recv_ref, direction_ref, residual_ref):
+def image_kernel(recv_ref, image_ref):
     coils = recv_ref.shape[0] // (ROWS * HALF)
     own = 2 * 96 // coils
     pieces = spread([load_rows(recv_ref, c, MESSAGE_IMAGE) for c in range(coils)], own, range(4))
-    for index, image_ref in enumerate((direction_ref, residual_ref)):
+    for index in range(2):
         (low0, high0), (low1, high1) = pieces[2 * index], pieces[2 * index + 1]
-        image_ref[0] = low0
-        image_ref[1] = low1
-        image_ref[2] = join_low(high0, high1)
+        image_ref[index, 0] = low0
+        image_ref[index, 1] = low1
+        image_ref[index, 2] = join_low(high0, high1)
 
 
 def normal_kernel(
@@ -147,11 +152,9 @@
     inv_y_ref,
     fwd_x_ref,
     inv_x_ref,
-    own_ref,
-    send_ref,
+    total_ref,
     line_ref,
     mid_ref,
-    total_ref,
     image_ref,
 ):
     coils = recv_ref.shape[0] // (ROWS * HALF)
@@ -160,8 +163,8 @@
     def load(c, slot):
         return load_rows(recv_ref, c, slot)
 
-    image_ref[core] = own_image_ref[...]
-    image_ref[1 - core] = other_image_ref[...]
+    image_ref[core] = own_image_ref[0]
+    image_ref[1 - core] = other_image_ref[0]
 
     def store_line(row, c, column, value):
         for term, half in enumerate(halves(value)):
@@ -230,42 +233,49 @@
             sum_im = sum_im + (s_re * y_im - s_im * y_re)
         total_ref[0, slot] = sum_re
         total_ref[1, slot] = sum_im
-    own_ref[...] = total_ref[core]
-    send_ref[...] = total_ref[1 - core]
-
-
-def finish_kernel(own_ref, other_ref, direction_ref, residual_ref, out_ref):
-    direction = direction_ref[...]
-    residual = residual_ref[...]
-    image_ap = own_ref[...] + other_ref[...] + damping_weight * direction
-    lane = lane_index(HALF)
-    coils = out_ref.shape[0] // HALF
-    own = 2 * 96 // coils
-    sums = jnp.zeros((HALF, LANES), jnp.float32)
-    products = (residual * residual, direction * image_ap, residual * image_ap, image_ap * image_ap)
-    for index, product in enumerate(products):
-        sums = jnp.where(lane == SUMS_AT + index, jnp.sum(product), sums)
-    high = image_ap[2]
-    for c in range(coils):
+
+
+def finish_kernel(core_ref, own_ref, other_ref, own_image_ref, other_image_ref, out_ref, total_ref):
+    core = core_ref[0]
+    part_sums = []
+    for part, image_ref in ((core, own_image_ref), (1 - core, other_image_ref)):
+        sums = [jnp.zeros((HALF, LANES), jnp.float32)] * 4
+        for slot in range(3):
+            direction, residual = image_ref[0, slot], image_ref[1, slot]
+            image_ap = own_ref[part, slot] + other_ref[part, slot] + damping_weight * direction
+            total_ref[part, slot] = image_ap
+            products = (residual * residual, direction * image_ap, residual * image_ap, image_ap * image_ap)
+            sums = [a + b for a, b in zip(sums, products)]
+        part_sums.append(sums)
+    sums = [a + b for a, b in zip(*part_sums)]
+    lane = lane_index(QUARTER)
+    message = jnp.zeros((QUARTER, LANES), jnp.float32)
+    for index, product in enumerate(sums):
+        message = jnp.where(lane == SUMS_AT + index, jnp.sum(product), message)
+    planes = out_ref.shape[0] // QUARTER
+    own = 2 * 96 // planes
+    rows = pl.ds(pl.multiple_of(core * QUARTER, QUARTER), QUARTER)
+    lines = [[total_ref[part, slot, rows, :] for slot in range(3)] for part in range(2)]
+    for c in range(planes):
         start = c * own
-        block = sums
-        for row in range(2):
-            at = row * own
-            inside = (lane >= at) & (lane < at + own)
-            if start < LANES:
-                block = jnp.where(inside, pltpu.roll(image_ap[row], (at - start) % LANES, 1), block)
-            if start + own > LANES:
-                moved = pltpu.roll(high, (at - (start - LANES + row * HALF)) % LANES, 1)
+        block = message
+        for part in range(2):
+            for row in range(2):
+                at = (2 * part + row) * own
+                inside = (lane >= at) & (lane < at + own)
                 if start < LANES:
-                    inside = inside & (lane >= at + LANES - start)
-                block = jnp.where(inside, moved, block)
-        out_ref[c * HALF : (c + 1) * HALF, :] = block
+                    block = jnp.where(inside, pltpu.roll(lines[part][row], (at - start) % LANES, 1), block)
+                if start + own > LANES:
+                    moved = pltpu.roll(lines[part][2], (at - (start - LANES + row * HALF)) % LANES, 1)
+                    if start < LANES:
+                        inside = inside & (lane >= at + LANES - start)
+                    block = jnp.where(inside, moved, block)
+        out_ref[c * QUARTER : (c + 1) * QUARTER, :] = block
 
 
 def update_kernel(
     recv_ref, solution_ref, residual_ref, direction_ref, next_solution_ref, next_residual_ref, next_direction_ref
 ):
-    cells = recv_ref.shape[0] // 2
     own = direction_ref.shape[3]
     totals = jnp.sum(recv_ref[...], axis=0, keepdims=True)
     lane = lax.broadcasted_iota(jnp.int32, (1, LANES), 1)
@@ -277,10 +287,11 @@
     alpha = norm_now / curvature
     fresh = jnp.maximum(norm_now + alpha * (alpha * square - 2.0 * cross), 0.0)
     beta = fresh / norm_now
+    turned = recv_ref[...].T
     for part in range(2):
-        turned = recv_ref[pl.ds(part, cells, stride=2), :].T
         for row in range(2):
-            image_ap = turned[row * own : (row + 1) * own]
+            at = (2 * part + row) * own
+            image_ap = turned[at : at + own]
             direction = direction_ref[part, 0, row]
             next_residual = residual_ref[part, 0, row] - alpha * image_ap
             next_solution_ref[part, 0, row] = solution_ref[part, 0, row] + alpha * direction
@@ -293,12 +304,11 @@
         pltpu.VMEM((2, 2, planes * HALF, 3 * LANES), jnp.bfloat16),
         pltpu.VMEM((2, planes, LANES, 3 * LANES), jnp.bfloat16),
         pltpu.VMEM((2, 3, HALF, LANES), jnp.float32),
-        pltpu.VMEM((2, 3, HALF, LANES), jnp.float32),
     ]
 
 
 def body(solution, residual, direction, sens_maps, sampling):
-    axes = ("coil", "slab")
+    axes = ("coil", "core", "chip")
     devices = lax.axis_size(axes)
     planes = lax.axis_size("coil")
     f32 = jnp.float32
@@ -314,33 +324,35 @@
         compiler_params=params,
         name="pack",
     )(*(pltpu.with_memory_space_constraint(a, pltpu.HBM) for a in (sens_maps, direction, residual)))
-    core = (lax.axis_index("slab") % 2).astype(jnp.int32).reshape(1)
+    core = lax.axis_index("core").astype(jnp.int32).reshape(1)
     packed, core = lax.optimization_barrier((packed, core))
     moved = lax.all_to_all(packed.reshape(devices * ROWS, 1, LANES), axes, 0, 0, tiled=True)
     moved = moved.reshape(devices * ROWS, LANES)
     tables = [jnp.asarray(t) for t in make_tables(sampling.shape[1], sampling.shape[2])]
-    swap = [(i, i ^ 1) for i in range(lax.axis_size("slab"))]
-    part = jax.ShapeDtypeStruct((3, HALF, LANES), f32)
-    image, residual_image = pl.pallas_call(
-        image_kernel, out_shape=(part, part), compiler_params=params, name="image"
-    )(moved)
-    other_image = lax.ppermute(image, "slab", swap)
-    own, send = pl.pallas_call(
+    swap = [(0, 1), (1, 0)]
+    both = jax.ShapeDtypeStruct((2, 3, HALF, LANES), f32)
+    image = pl.pallas_call(image_kernel, out_shape=both, compiler_params=params, name="image")(moved)
+    other_image = lax.ppermute(image, "core", swap)
+    scalar = pl.BlockSpec(memory_space=pltpu.SMEM)
+    own = pl.pallas_call(
         normal_kernel,
-        in_specs=[pl.BlockSpec(memory_space=pltpu.SMEM)] + [whole] * (4 + len(tables)),
-        out_shape=(part, part),
+        in_specs=[scalar] + [whole] * (4 + len(tables)),
+        out_shape=both,
         scratch_shapes=normal_scratch(planes),
         compiler_params=params,
         name="normal",
     )(core, moved, image, other_image, sampling[0].T, *tables)
-    other = lax.ppermute(send, "slab", swap)
+    other = lax.ppermute(own, "core", swap)
+    chips = devices // 2
     result = pl.pallas_call(
         finish_kernel,
-        out_shape=jax.ShapeDtypeStruct((devices, LANES), f32),
+        in_specs=[scalar] + [whole] * 4,
+        out_shape=jax.ShapeDtypeStruct((chips, LANES), f32),
+        scratch_shapes=[pltpu.VMEM(both.shape, f32)],
         compiler_params=params,
         name="finish",
-    )(own, other, image, residual_image)
-    home = lax.all_to_all(result.reshape(devices, 1, LANES), axes, 0, 0, tiled=True).reshape(devices, LANES)
+    )(core, own, other, image, other_image)
+    home = lax.all_to_all(result.reshape(chips, 1, LANES), ("coil", "chip"), 0, 0, tiled=True).reshape(chips, LANES)
     out = jax.ShapeDtypeStruct(direction.shape, f32)
     return tuple(
         pl.pallas_call(update_kernel, out_shape=(out, out, out), compiler_params=params, name="update")(
@@ -350,6 +362,8 @@
 
 
 def solution(mesh):
-    image = P(None, None, "slab", "coil", None)
-    in_specs = (image, image, image, P(None, "coil", "slab", None, None), P())
-    return jax.shard_map(body, mesh=mesh, in_specs=in_specs, out_specs=(image, image, image), check_vma=False)
+    planes, slabs = mesh.devices.shape
+    split = Mesh(mesh.devices.reshape(planes, slabs // 2, 2), ("coil", "chip", "core"))
+    image = P(None, None, ("chip", "core"), "coil", None)
+    in_specs = (image, image, image, P(None, "coil", ("chip", "core"), None, None), P())
+    return jax.shard_map(body, mesh=split, in_specs=in_specs, out_specs=(image, image, image), check_vma=False)

time: 116 us -> 112 us (0.966)
  blocking collectives: 97 us -> 93.2 us
    all_to_all x1, blocking collectives: 26.7 us -> 21.1 us  [body(): lax.all_to_all(result.reshape(chips, 1, LANES), ('coil', 'chip'), 0, 0, t...]
    all_to_all x1, blocking collectives: 70.4 us -> 72.1 us  [body(): lax.all_to_all(packed.reshape(devices * ROWS, 1, LANES), axes, 0, 0, tile...]
where the time goes in v5:
time: 112 us
  blocking collectives  93.2 us (83%)
  Pallas kernels  9.95 us (9%)
  starting transfers between devices  5.76 us (5%)
  waiting for transfers between devices  2.1 us (2%)
    all_to_all x1, blocking collectives, body(): lax.all_to_all(packed.reshape(devices * ROWS, 1, LANES), axes, 0, 0, tile...  72.1 us
    all_to_all x1, blocking collectives, body(): lax.all_to_all(result.reshape(chips, 1, LANES), ('coil', 'chip'), 0, 0, t...  21.1 us
    pallas_call x1, Pallas kernels, body(): pl.pallas_call(normal_kernel, in_specs=[scalar] + [whole] * (4 + len(tabl...  6.31 us
    ppermute x1, starting transfers between devices, body(): other_image = lax.ppermute(image, 'core', swap)  3.47 us
    ppermute x1, starting transfers between devices, body(): other = lax.ppermute(own, 'core', swap)  2.29 us
  transfers between devices with their start and end apart: 2, of which 2 were waited for; matrix products, arithmetic and copies ran while one was open for 0% of the time, Pallas kernels for 0%

profile of v5, /device:TPU:1, one launch (start us, length us, event | category | flops | bytes accessed | tf_op | source)
XLA Modules:
  0.0 111.8 jit_solution(18278085317381614118)
XLA Ops:
  0.6 2.1 %pack.1 = f32[3584,128]{1,0:T(8,128)S(1)} custom-call(f32[2,2,2,192,256]{4,3,2,1,0:T(8,128)} %maps_hbm.1, f32[2,1,2,24,256]{4,3,2,1,0:T(8,128)} %direction_ref.1, f32[2,1,2,24,256]{4,3,2,1,0:T(8,128)} %residual_ref.1), custom_call_target="tpu_custom_call" | custom-call | tf_op jit(solution)/shard_map/pack/pallas_call | solution.py:318
  2.8 72.1 %all_to_all.10 = f32[3584,1,128]{2,1,0:T(1,128)S(1)} all-to-all(f32[3584,1,128]{2,1,0:T(1,128)S(1)} %bitcast.14), channel_id=1, replica_groups=mesh['coil'=8,'chip'=32,'core'=2] {'coil','core','chip'}, dimensions={0} | all-to-all | bytes 3670016 | tf_op jit(solution)/shard_map/all_to_all | solution.py:329
  74.9 0.0 copy-start
  74.9 0.0 copy-start.1
  74.9 0.0 copy-start.4
  74.9 0.0 copy-start.5
  74.9 0.0 copy-start.7
  74.9 0.3 image.1.own_image_ref
  75.2 3.5 %collective-permute-start = (f32[2,3,64,128]{3,2,1,0:T(8,128)S(1)}, f32[2,3,64,128]{3,2,1,0:T(8,128)S(1)}, u32[]{:S(2)}, u32[]{:S(2)}) collective-permute-start(f32[2,3,64,128]{3,2,1,0:T(8,128)S(1)} %image.1.own_image_ref), channel_id=1, source_target_pairs={{0,1},{1,0},{2,3},{3,2},{4,5},{5,4},{6,7},{7,6},{8,9},{9,8},{10,11... | collective-permute-start | bytes 589832 | tf_op jit(solution)/shard_map/ppermute | solution.py:335
  78.7 1.0 collective-permute-done.other_image_ref
  79.8 0.0 copy-done
  79.8 0.0 copy-done.1
  79.8 0.0 copy-done.4
  79.8 0.0 copy-done.5
  79.8 0.0 copy-done.7
  79.8 0.0 copy-start.2
  79.8 0.0 copy-start.3
  79.8 0.0 copy-start.6
  79.8 6.3 %normal.1.own_ref = f32[2,3,64,128]{3,2,1,0:T(8,128)S(1)} custom-call(s32[1]{0:T(128)} %bitcast.core_ref, f32[3584,128]{1,0:T(8,128)S(1)} %bitcast.13, f32[2,3,64,128]{3,2,1,0:T(8,128)S(1)} %image.1.own_image_ref, f32[2,3,64,128]{3,2,1,0:T(8,128)S(1)} %collective-permute-done.other_image_ref, s32[192,128]{1,0:T(8,128)S(1)} %bitcast.17, ...), custom_call_target="tpu_custom_call" | custom-call | tf_op jit(solution)/shard_map/normal/pallas_call | solution.py:337
  86.1 2.3 %collective-permute-start.1 = (f32[2,3,64,128]{3,2,1,0:T(8,128)S(1)}, f32[2,3,64,128]{3,2,1,0:T(8,128)S(1)}, u32[]{:S(2)}, u32[]{:S(2)}) collective-permute-start(f32[2,3,64,128]{3,2,1,0:T(8,128)S(1)} %normal.1.own_ref), channel_id=1, source_target_pairs={{0,1},{1,0},{2,3},{3,2},{4,5},{5,4},{6,7},{7,6},{8,9},{9,8},{10,11... | collective-permute-start | bytes 589832 | tf_op jit(solution)/shard_map/ppermute | solution.py:345
  88.4 1.0 collective-permute-done.1.other_ref
  89.5 0.3 finish.1
  89.8 21.1 %all_to_all.11 = f32[256,1,128]{2,1,0:T(1,128)S(1)} all-to-all(f32[256,1,128]{2,1,0:T(1,128)S(1)} %bitcast.15), channel_id=1, replica_groups=mesh['coil'=8,'chip'=32,'core'=2] {'coil','chip'}, dimensions={0} | all-to-all | bytes 262144 | tf_op jit(solution)/shard_map/all_to_all | solution.py:355
  110.9 0.0 copy-done.2
  110.9 0.0 copy-done.3
  110.9 0.0 copy-done.6
  111.0 0.8 update.1
Async XLA Ops:
  74.9 4.9 %copy-start = (bf16[2,384,384]{2,1,0:T(8,128)(2,1)S(1)}, bf16[2,384,384]{2,1,0:T(8,128)(2,1)}, u32[]{:S(2)}) copy-start(bf16[2,384,384]{2,1,0:T(8,128)(2,1)} %constant.13.clone.inv_y_ref) | copy-start | bytes 1769476
  74.9 4.9 %copy-start.1 = (bf16[2,384,384]{2,1,0:T(8,128)(2,1)S(1)}, bf16[2,384,384]{2,1,0:T(8,128)(2,1)}, u32[]{:S(2)}) copy-start(bf16[2,384,384]{2,1,0:T(8,128)(2,1)} %constant.12.clone.fwd_y_ref) | copy-start | bytes 1769476
  74.9 4.9 %copy-start.4 = (bf16[2,256,128]{2,1,0:T(8,128)(2,1)S(1)}, bf16[2,256,128]{2,1,0:T(8,128)(2,1)}, u32[]{:S(2)}) copy-start(bf16[2,256,128]{2,1,0:T(8,128)(2,1)} %constant.15.clone.inv_x_ref) | copy-start | bytes 393220
  74.9 4.9 %copy-start.5 = (bf16[2,256,128]{2,1,0:T(8,128)(2,1)S(1)}, bf16[2,256,128]{2,1,0:T(8,128)(2,1)}, u32[]{:S(2)}) copy-start(bf16[2,256,128]{2,1,0:T(8,128)(2,1)} %constant.14.clone.fwd_x_ref) | copy-start | bytes 393220
  74.9 4.9 %copy-start.7 = (s32[1,128,192]{1,2,0:T(8,128)S(1)}, s32[1,128,192]{1,2,0:T(8,128)}, u32[]{:S(2)}) copy-start(s32[1,128,192]{1,2,0:T(8,128)} %param.13) | copy-start | bytes 294916
  75.2 4.5 %collective-permute-start = (f32[2,3,64,128]{3,2,1,0:T(8,128)S(1)}, f32[2,3,64,128]{3,2,1,0:T(8,128)S(1)}, u32[]{:S(2)}, u32[]{:S(2)}) collective-permute-start(f32[2,3,64,128]{3,2,1,0:T(8,128)S(1)} %image.1.own_image_ref), channel_id=1, source_target_pairs={{0,1},{1,0},{2,3},{3,2},{4,5},{5,4},{6,7},{7,6},{8,9},{9,8},{10,11... | collective-permute-start | bytes 589832 | tf_op jit(solution)/shard_map/ppermute | solution.py:335
  79.8 31.2 %copy-start.2 = (f32[2,1,2,24,256]{4,3,2,1,0:T(8,128)S(1)}, f32[2,1,2,24,256]{4,3,2,1,0:T(8,128)}, u32[]{:S(2)}) copy-start(f32[2,1,2,24,256]{4,3,2,1,0:T(8,128)} %direction_ref.1) | copy-start | bytes 294916
  79.8 31.1 %copy-start.3 = (f32[2,1,2,24,256]{4,3,2,1,0:T(8,128)S(1)}, f32[2,1,2,24,256]{4,3,2,1,0:T(8,128)}, u32[]{:S(2)}) copy-start(f32[2,1,2,24,256]{4,3,2,1,0:T(8,128)} %residual_ref.1) | copy-start | bytes 294916
  79.8 31.1 %copy-start.6 = (f32[2,1,2,24,256]{4,3,2,1,0:T(8,128)S(1)}, f32[2,1,2,24,256]{4,3,2,1,0:T(8,128)}, u32[]{:S(2)}) copy-start(f32[2,1,2,24,256]{4,3,2,1,0:T(8,128)} %solution_ref.1) | copy-start | bytes 294916
  86.1 3.3 %collective-permute-start.1 = (f32[2,3,64,128]{3,2,1,0:T(8,128)S(1)}, f32[2,3,64,128]{3,2,1,0:T(8,128)S(1)}, u32[]{:S(2)}, u32[]{:S(2)}) collective-permute-start(f32[2,3,64,128]{3,2,1,0:T(8,128)S(1)} %normal.1.own_ref), channel_id=1, source_target_pairs={{0,1},{1,0},{2,3},{3,2},{4,5},{5,4},{6,7},{7,6},{8,9},{9,8},{10,11... | collective-permute-start | bytes 589832 | tf_op jit(solution)/shard_map/ppermute | solution.py:345

commit v6 on v5

--- a/solution.py
+++ b/solution.py
@@ -40,17 +40,17 @@
     re_from_im = np.concatenate([sin_y[:, :LANES], cos_y[:, :LANES], sin_y[:, LANES:], cos_y[:, LANES:]], axis=1)
     fwd_y = np.concatenate([re_from_re[:LANES], re_from_im[:LANES], re_from_re[LANES:], re_from_im[LANES:]], axis=0)
     order = np.arange(size_x).reshape(-1, 2, 2).transpose(2, 1, 0).reshape(-1)
-    fwd_x = np.concatenate([cos_x[:, order], sin_x[:, order]], axis=0)
-    inv_x = np.concatenate([cos_x[order], sin_x[order]], axis=0)
-    return [split_pair(t) for t in (fwd_y, fwd_y.T, fwd_x, inv_x)]
+    fwd_x = np.block([[cos_x[:, order], sin_x[:, order]], [-sin_x[:, order], cos_x[:, order]]])
+    return [split_pair(t) for t in (fwd_y, fwd_y.T, fwd_x, fwd_x.T)]
 
 
 def pack_kernel(maps_hbm, direction_hbm, residual_hbm, out_ref, maps_ref, direction_ref, residual_ref, maps_sem, image_sem):
     cells = maps_ref.shape[4]
     copies = [
-        pltpu.make_async_copy(maps_hbm.at[part, core], maps_ref.at[part, core], maps_sem.at[part, core])
+        pltpu.make_async_copy(maps_hbm.at[part, core, row], maps_ref.at[part, core, row], maps_sem.at[part, core, row])
         for core in range(2)
         for part in range(2)
+        for row in range(2)
     ]
     images = [
         pltpu.make_async_copy(direction_hbm, direction_ref, image_sem.at[0]),
@@ -74,8 +74,8 @@
         put(core, MESSAGE_IMAGE, jnp.concatenate(pieces + [filler], axis=0))
     for core in range(2):
         for part in range(2):
-            copies[core * 2 + part].wait()
             for row in range(2):
+                copies[core * 4 + part * 2 + row].wait()
                 put(core, part * 2 + row, maps_ref[part, core, row, :LANES, :])
             put(
                 core,
@@ -120,11 +120,8 @@
     return high, low
 
 
-def dot3(left_high, left_low, right_high, right_low):
-    def dot(a, b):
-        return jnp.dot(a, b, preferred_element_type=jnp.float32)
-
-    return dot(left_high, right_high) + (dot(left_high, right_low) + dot(left_low, right_high))
+def dot(a, b):
+    return jnp.dot(a, b, preferred_element_type=jnp.float32)
 
 
 def load_rows(recv_ref, c, slot):
@@ -168,7 +165,12 @@
 
     def store_line(row, c, column, value):
         for term, half in enumerate(halves(value)):
-            line_ref[term, row, c * HALF : (c + 1) * HALF, column * LANES : (column + 1) * LANES] = half
+            at = (term * 3 + column) * LANES
+            line_ref[row, c * HALF : (c + 1) * HALF, at : at + LANES] = half
+
+    def along_y(row, table_ref):
+        twice = jnp.concatenate([table_ref[0], table_ref[0]], axis=0)
+        return dot(line_ref[row], twice) + dot(line_ref[row, :, : 3 * LANES], table_ref[1])
 
     for c in range(coils):
         for slot in range(3):
@@ -184,39 +186,37 @@
                 store_line(0, c, 2, join_low(x_re, x_im))
                 store_line(1, c, 2, join_high(x_re, x_im))
     for row in range(2):
-        spectra = dot3(line_ref[0, row], line_ref[1, row], fwd_y_ref[0], fwd_y_ref[1])
-        for term, half in enumerate(halves(spectra)):
-            for c in range(coils):
-                mid_ref[term, c, row * HALF : (row + 1) * HALF, :] = half[c * HALF : (c + 1) * HALF]
+        spectra = along_y(row, fwd_y_ref)
+        for pair in range(coils // 2):
+            first, second = (spectra[c * HALF : (c + 1) * HALF] for c in (2 * pair, 2 * pair + 1))
+            mixes = first[:, 2 * LANES :], second[:, 2 * LANES :]
+            for part, join in enumerate((join_low, join_high)):
+                at = (2 * part + row) * HALF
+                columns = (
+                    first[:, part * LANES : (part + 1) * LANES],
+                    second[:, part * LANES : (part + 1) * LANES],
+                    join(*mixes),
+                )
+                for column, value in enumerate(columns):
+                    for term, half in enumerate(halves(value)):
+                        mid_ref[term, pair, at : at + HALF, column * LANES : (column + 1) * LANES] = half
     weight_low = weight_ref[:LANES].astype(jnp.float32).T
     weight_high = weight_ref[LANES:].astype(jnp.float32).T
-    weight_mix = jnp.concatenate([weight_high, weight_high], axis=1)
-    sign = jnp.where(lane_index(LANES) < HALF, 1.0, -1.0).astype(jnp.float32)
-    for c in range(coils):
-        both = dot3(fwd_x_ref[0], fwd_x_ref[1], mid_ref[0, c], mid_ref[1, c])
-        p, q = both[:LANES], both[LANES:]
-        turned = sign * pltpu.roll(q[:, 2 * LANES :], HALF, 1)
-        masked = jnp.concatenate(
-            [
-                (p[:, :LANES] + q[:, LANES : 2 * LANES]) * weight_low,
-                (p[:, LANES : 2 * LANES] - q[:, :LANES]) * weight_low,
-                (p[:, 2 * LANES :] + turned) * weight_mix,
-            ],
-            axis=1,
-        )
-        masked_high, masked_low = halves(masked)
-        both = dot3(inv_x_ref[0], inv_x_ref[1], masked_high, masked_low)
-        p, q = both[:LANES], both[LANES:]
-        turned = sign * pltpu.roll(q[:, 2 * LANES :], HALF, 1)
-        columns = (
-            p[:, :LANES] - q[:, LANES : 2 * LANES],
-            p[:, LANES : 2 * LANES] + q[:, :LANES],
-            p[:, 2 * LANES :] - turned,
-        )
-        for column, value in enumerate(columns):
-            for row in range(2):
-                store_line(row, c, column, value[row * HALF : (row + 1) * HALF])
-    lines = [dot3(line_ref[0, row], line_ref[1, row], inv_y_ref[0], inv_y_ref[1]) for row in range(2)]
+    weight = jnp.concatenate([weight_low, weight_low, jnp.concatenate([weight_high, weight_high], axis=1)], axis=1)
+    weight = jnp.concatenate([weight, weight], axis=0)
+    for pair in range(coils // 2):
+        high, low = mid_ref[0, pair], mid_ref[1, pair]
+        spectra = dot(fwd_x_ref[0], high) + (dot(fwd_x_ref[0], low) + dot(fwd_x_ref[1], high))
+        high, low = halves(spectra * weight)
+        value = dot(inv_x_ref[0], high) + (dot(inv_x_ref[0], low) + dot(inv_x_ref[1], high))
+        for row in range(2):
+            re, im = (value[(2 * part + row) * HALF : (2 * part + row + 1) * HALF] for part in range(2))
+            mixes = re[:, 2 * LANES :], im[:, 2 * LANES :]
+            for index, join in enumerate((join_low, join_high)):
+                store_line(row, 2 * pair + index, 0, re[:, index * LANES : (index + 1) * LANES])
+                store_line(row, 2 * pair + index, 1, im[:, index * LANES : (index + 1) * LANES])
+                store_line(row, 2 * pair + index, 2, join(*mixes))
+    lines = [along_y(row, inv_y_ref) for row in range(2)]
     for slot in range(3):
         sum_re = jnp.zeros((HALF, LANES), jnp.float32)
         sum_im = jnp.zeros((HALF, LANES), jnp.float32)
@@ -301,8 +301,8 @@
 
 def normal_scratch(planes):
     return [
-        pltpu.VMEM((2, 2, planes * HALF, 3 * LANES), jnp.bfloat16),
-        pltpu.VMEM((2, planes, LANES, 3 * LANES), jnp.bfloat16),
+        pltpu.VMEM((2, planes * HALF, 2 * 3 * LANES), jnp.bfloat16),
+        pltpu.VMEM((2, planes // 2, 2 * LANES, 3 * LANES), jnp.bfloat16),
         pltpu.VMEM((2, 3, HALF, LANES), jnp.float32),
     ]
 
@@ -320,7 +320,7 @@
         in_specs=[hbm] * 3,
         out_shape=jax.ShapeDtypeStruct((devices * ROWS, LANES), f32),
         scratch_shapes=[pltpu.VMEM(a.shape, f32) for a in (sens_maps, direction, residual)]
-        + [pltpu.SemaphoreType.DMA((2, 2)), pltpu.SemaphoreType.DMA((2,))],
+        + [pltpu.SemaphoreType.DMA((2, 2, 2)), pltpu.SemaphoreType.DMA((2,))],
         compiler_params=params,
         name="pack",
     )(*(pltpu.with_memory_space_constraint(a, pltpu.HBM) for a in (sens_maps, direction, residual)))

time: 112 us -> 111 us (level)
    pallas_call x1, Pallas kernels: 6.31 us -> 5.18 us  [body(): pl.pallas_call(normal_kernel, in_specs=[scalar] + [whole] * (4 + len(tabl...]
where the time goes in v6:
time: 111 us
  blocking collectives  93 us (84%)
  Pallas kernels  9.29 us (8%)
  starting transfers between devices  5.76 us (5%)
  waiting for transfers between devices  2.1 us (2%)
    all_to_all x1, blocking collectives, body(): lax.all_to_all(packed.reshape(devices * ROWS, 1, LANES), axes, 0, 0, tile...  72.1 us
    all_to_all x1, blocking collectives, body(): lax.all_to_all(result.reshape(chips, 1, LANES), ('coil', 'chip'), 0, 0, t...  21 us
    pallas_call x1, Pallas kernels, body(): pl.pallas_call(normal_kernel, in_specs=[scalar] + [whole] * (4 + len(tabl...  5.18 us
    ppermute x1, starting transfers between devices, body(): other_image = lax.ppermute(image, 'core', swap)  3.47 us
    pallas_call x1, Pallas kernels, body(): pl.pallas_call(pack_kernel, in_specs=[hbm] * 3, out_shape=jax.ShapeDtypeS...  2.62 us
    ppermute x1, starting transfers between devices, body(): other = lax.ppermute(own, 'core', swap)  2.29 us
  transfers between devices with their start and end apart: 2, of which 2 were waited for; matrix products, arithmetic and copies ran while one was open for 0% of the time, Pallas kernels for 0%

profile of v6, /device:TPU:1, one launch (start us, length us, event | category | flops | bytes accessed | tf_op | source)
XLA Modules:
  0.0 111.0 jit_solution(2526790466102832236)
XLA Ops:
  0.6 2.6 %pack.1 = f32[3584,128]{1,0:T(8,128)S(1)} custom-call(f32[2,2,2,192,256]{4,3,2,1,0:T(8,128)} %maps_hbm.1, f32[2,1,2,24,256]{4,3,2,1,0:T(8,128)} %direction_ref.1, f32[2,1,2,24,256]{4,3,2,1,0:T(8,128)} %residual_ref.1), custom_call_target="tpu_custom_call" | custom-call | tf_op jit(solution)/shard_map/pack/pallas_call | solution.py:318
  3.3 72.1 %all_to_all.10 = f32[3584,1,128]{2,1,0:T(1,128)S(1)} all-to-all(f32[3584,1,128]{2,1,0:T(1,128)S(1)} %bitcast.14), channel_id=1, replica_groups=mesh['coil'=8,'chip'=32,'core'=2] {'coil','core','chip'}, dimensions={0} | all-to-all | bytes 3670016 | tf_op jit(solution)/shard_map/all_to_all | solution.py:329
  75.3 0.0 copy-start
  75.4 0.0 copy-start.1
  75.4 0.0 copy-start.4
  75.4 0.0 copy-start.5
  75.4 0.0 copy-start.7
  75.4 0.3 image.1.own_image_ref
  75.7 3.5 %collective-permute-start = (f32[2,3,64,128]{3,2,1,0:T(8,128)S(1)}, f32[2,3,64,128]{3,2,1,0:T(8,128)S(1)}, u32[]{:S(2)}, u32[]{:S(2)}) collective-permute-start(f32[2,3,64,128]{3,2,1,0:T(8,128)S(1)} %image.1.own_image_ref), channel_id=1, source_target_pairs={{0,1},{1,0},{2,3},{3,2},{4,5},{5,4},{6,7},{7,6},{8,9},{9,8},{10,11... | collective-permute-start | bytes 589832 | tf_op jit(solution)/shard_map/ppermute | solution.py:335
  79.2 1.0 collective-permute-done.other_image_ref
  80.2 0.0 copy-done
  80.2 0.0 copy-done.1
  80.2 0.0 copy-done.4
  80.2 0.0 copy-done.5
  80.3 0.0 copy-done.7
  80.3 0.0 copy-start.2
  80.3 0.0 copy-start.3
  80.3 0.0 copy-start.6
  80.3 5.2 %normal.1.own_ref = f32[2,3,64,128]{3,2,1,0:T(8,128)S(1)} custom-call(s32[1]{0:T(128)} %bitcast.core_ref, f32[3584,128]{1,0:T(8,128)S(1)} %bitcast.13, f32[2,3,64,128]{3,2,1,0:T(8,128)S(1)} %image.1.own_image_ref, f32[2,3,64,128]{3,2,1,0:T(8,128)S(1)} %collective-permute-done.other_image_ref, s32[192,128]{1,0:T(8,128)S(1)} %bitcast.17, ...), custom_call_target="tpu_custom_call" | custom-call | tf_op jit(solution)/shard_map/normal/pallas_call | solution.py:337
  85.5 2.3 %collective-permute-start.1 = (f32[2,3,64,128]{3,2,1,0:T(8,128)S(1)}, f32[2,3,64,128]{3,2,1,0:T(8,128)S(1)}, u32[]{:S(2)}, u32[]{:S(2)}) collective-permute-start(f32[2,3,64,128]{3,2,1,0:T(8,128)S(1)} %normal.1.own_ref), channel_id=1, source_target_pairs={{0,1},{1,0},{2,3},{3,2},{4,5},{5,4},{6,7},{7,6},{8,9},{9,8},{10,11... | collective-permute-start | bytes 589832 | tf_op jit(solution)/shard_map/ppermute | solution.py:345
  87.8 1.0 collective-permute-done.1.other_ref
  88.8 0.3 finish.1
  89.1 21.0 %all_to_all.11 = f32[256,1,128]{2,1,0:T(1,128)S(1)} all-to-all(f32[256,1,128]{2,1,0:T(1,128)S(1)} %bitcast.15), channel_id=1, replica_groups=mesh['coil'=8,'chip'=32,'core'=2] {'coil','chip'}, dimensions={0} | all-to-all | bytes 262144 | tf_op jit(solution)/shard_map/all_to_all | solution.py:355
  110.1 0.0 copy-done.2
  110.1 0.0 copy-done.3
  110.1 0.0 copy-done.6
  110.1 0.8 update.1
Async XLA Ops:
  75.3 4.9 %copy-start = (bf16[2,384,384]{2,1,0:T(8,128)(2,1)S(1)}, bf16[2,384,384]{2,1,0:T(8,128)(2,1)}, u32[]{:S(2)}) copy-start(bf16[2,384,384]{2,1,0:T(8,128)(2,1)} %constant.13.clone.inv_y_ref) | copy-start | bytes 1769476
  75.4 4.9 %copy-start.1 = (bf16[2,384,384]{2,1,0:T(8,128)(2,1)S(1)}, bf16[2,384,384]{2,1,0:T(8,128)(2,1)}, u32[]{:S(2)}) copy-start(bf16[2,384,384]{2,1,0:T(8,128)(2,1)} %constant.12.clone.fwd_y_ref) | copy-start | bytes 1769476
  75.4 4.9 %copy-start.4 = (bf16[2,256,256]{2,1,0:T(8,128)(2,1)S(1)}, bf16[2,256,256]{2,1,0:T(8,128)(2,1)}, u32[]{:S(2)}) copy-start(bf16[2,256,256]{2,1,0:T(8,128)(2,1)} %constant.15.clone.inv_x_ref) | copy-start | bytes 786436
  75.4 4.9 %copy-start.5 = (bf16[2,256,256]{2,1,0:T(8,128)(2,1)S(1)}, bf16[2,256,256]{2,1,0:T(8,128)(2,1)}, u32[]{:S(2)}) copy-start(bf16[2,256,256]{2,1,0:T(8,128)(2,1)} %constant.14.clone.fwd_x_ref) | copy-start | bytes 786436
  75.4 4.9 %copy-start.7 = (s32[1,128,192]{1,2,0:T(8,128)S(1)}, s32[1,128,192]{1,2,0:T(8,128)}, u32[]{:S(2)}) copy-start(s32[1,128,192]{1,2,0:T(8,128)} %param.13) | copy-start | bytes 294916
  75.7 4.5 %collective-permute-start = (f32[2,3,64,128]{3,2,1,0:T(8,128)S(1)}, f32[2,3,64,128]{3,2,1,0:T(8,128)S(1)}, u32[]{:S(2)}, u32[]{:S(2)}) collective-permute-start(f32[2,3,64,128]{3,2,1,0:T(8,128)S(1)} %image.1.own_image_ref), channel_id=1, source_target_pairs={{0,1},{1,0},{2,3},{3,2},{4,5},{5,4},{6,7},{7,6},{8,9},{9,8},{10,11... | collective-permute-start | bytes 589832 | tf_op jit(solution)/shard_map/ppermute | solution.py:335
  80.3 29.8 %copy-start.2 = (f32[2,1,2,24,256]{4,3,2,1,0:T(8,128)S(1)}, f32[2,1,2,24,256]{4,3,2,1,0:T(8,128)}, u32[]{:S(2)}) copy-start(f32[2,1,2,24,256]{4,3,2,1,0:T(8,128)} %direction_ref.1) | copy-start | bytes 294916
  80.3 29.8 %copy-start.3 = (f32[2,1,2,24,256]{4,3,2,1,0:T(8,128)S(1)}, f32[2,1,2,24,256]{4,3,2,1,0:T(8,128)}, u32[]{:S(2)}) copy-start(f32[2,1,2,24,256]{4,3,2,1,0:T(8,128)} %residual_ref.1) | copy-start | bytes 294916
  80.3 29.8 %copy-start.6 = (f32[2,1,2,24,256]{4,3,2,1,0:T(8,128)S(1)}, f32[2,1,2,24,256]{4,3,2,1,0:T(8,128)}, u32[]{:S(2)}) copy-start(f32[2,1,2,24,256]{4,3,2,1,0:T(8,128)} %solution_ref.1) | copy-start | bytes 294916
  85.5 3.3 %collective-permute-start.1 = (f32[2,3,64,128]{3,2,1,0:T(8,128)S(1)}, f32[2,3,64,128]{3,2,1,0:T(8,128)S(1)}, u32[]{:S(2)}, u32[]{:S(2)}) collective-permute-start(f32[2,3,64,128]{3,2,1,0:T(8,128)S(1)} %normal.1.own_ref), channel_id=1, source_target_pairs={{0,1},{1,0},{2,3},{3,2},{4,5},{5,4},{6,7},{7,6},{8,9},{9,8},{10,11... | collective-permute-start | bytes 589832 | tf_op jit(solution)/shard_map/ppermute | solution.py:345

commit v7 on v6

--- a/solution.py
+++ b/solution.py
@@ -41,22 +41,20 @@
     fwd_y = np.concatenate([re_from_re[:LANES], re_from_im[:LANES], re_from_re[LANES:], re_from_im[LANES:]], axis=0)
     order = np.arange(size_x).reshape(-1, 2, 2).transpose(2, 1, 0).reshape(-1)
     fwd_x = np.block([[cos_x[:, order], sin_x[:, order]], [-sin_x[:, order], cos_x[:, order]]])
+    fwd_x = fwd_x.reshape(2 * size_x, 2, 2, HALF).transpose(0, 2, 1, 3).reshape(2 * size_x, 2 * size_x)
     return [split_pair(t) for t in (fwd_y, fwd_y.T, fwd_x, fwd_x.T)]
 
 
 def pack_kernel(maps_hbm, direction_hbm, residual_hbm, out_ref, maps_ref, direction_ref, residual_ref, maps_sem, image_sem):
     cells = maps_ref.shape[4]
     copies = [
-        pltpu.make_async_copy(maps_hbm.at[part, core, row], maps_ref.at[part, core, row], maps_sem.at[part, core, row])
-        for core in range(2)
-        for part in range(2)
-        for row in range(2)
+        pltpu.make_async_copy(maps_hbm.at[:, core], maps_ref.at[:, core], maps_sem.at[core]) for core in range(2)
     ]
     images = [
         pltpu.make_async_copy(direction_hbm, direction_ref, image_sem.at[0]),
         pltpu.make_async_copy(residual_hbm, residual_ref, image_sem.at[1]),
     ]
-    for copy in images + copies:
+    for copy in copies + images:
         copy.start()
 
     def put(core, slot, block):
@@ -65,23 +63,23 @@
             rows = pl.ds((plane * HALF + core * QUARTER) * ROWS + slot, QUARTER, stride=ROWS)
             out_ref[rows, :] = turned[plane * QUARTER : (plane + 1) * QUARTER]
 
-    for copy in images:
-        copy.wait()
-    own = direction_ref.shape[3]
-    filler = jnp.zeros((LANES - 4 * own, cells), jnp.float32)
     for core in range(2):
-        pieces = [image_ref[core, 0, row] for image_ref in (direction_ref, residual_ref) for row in range(2)]
-        put(core, MESSAGE_IMAGE, jnp.concatenate(pieces + [filler], axis=0))
-    for core in range(2):
+        copies[core].wait()
         for part in range(2):
             for row in range(2):
-                copies[core * 4 + part * 2 + row].wait()
                 put(core, part * 2 + row, maps_ref[part, core, row, :LANES, :])
             put(
                 core,
                 4 + part,
                 jnp.concatenate([maps_ref[part, core, 0, LANES:, :], maps_ref[part, core, 1, LANES:, :]], axis=0),
             )
+    for copy in images:
+        copy.wait()
+    filler = jnp.zeros((LANES - 5 * direction_ref.shape[3], cells), jnp.float32)
+    for core in range(2):
+        pieces = [direction_ref[0, 0, 0], direction_ref[1, 0, 0], direction_ref[core, 0, 1]]
+        pieces += [residual_ref[core, 0, 0], residual_ref[core, 0, 1], filler]
+        put(core, MESSAGE_IMAGE, jnp.concatenate(pieces, axis=0))
 
 
 def lane_index(rows):
@@ -128,22 +126,69 @@
     return recv_ref[pl.ds(c * HALF * ROWS + slot, HALF, stride=ROWS), :]
 
 
-def image_kernel(recv_ref, image_ref):
+def image_kernel(recv_ref, first_ref, rest_ref):
     coils = recv_ref.shape[0] // (ROWS * HALF)
     own = 2 * 96 // coils
-    pieces = spread([load_rows(recv_ref, c, MESSAGE_IMAGE) for c in range(coils)], own, range(4))
-    for index in range(2):
-        (low0, high0), (low1, high1) = pieces[2 * index], pieces[2 * index + 1]
-        image_ref[index, 0] = low0
-        image_ref[index, 1] = low1
-        image_ref[index, 2] = join_low(high0, high1)
+    lines = spread([load_rows(recv_ref, c, MESSAGE_IMAGE) for c in range(coils)], own, range(5))
+    for part in range(2):
+        for index in range(2):
+            first_ref[part, index] = lines[part][index]
+    for index in range(3):
+        rest_ref[index] = lines[2 + index][0]
+    rest_ref[3] = join_low(lines[3][1], lines[4][1])
+    rest_ref[4] = pltpu.roll(lines[2][1], HALF, 1)
+
+
+def store_halves(line_ref, c, column, value):
+    for term, half in enumerate(halves(value)):
+        at = (term * 3 + column) * LANES
+        line_ref[c * HALF : (c + 1) * HALF, at : at + LANES] = half
+
+
+def along_y(line_ref, table_ref):
+    twice = jnp.concatenate([table_ref[0], table_ref[0]], axis=0)
+    return dot(line_ref[...], twice) + dot(line_ref[:, : 3 * LANES], table_ref[1])
+
+
+def forward_y(recv_ref, row, image_ref, table_ref, line_ref, mid_ref):
+    coils = recv_ref.shape[0] // (ROWS * HALF)
+    join = join_high if row else join_low
+    for c in range(coils):
+        products = []
+        for index, slot in enumerate((row, 4)):
+            s_re = load_rows(recv_ref, c, slot)
+            s_im = load_rows(recv_ref, c, slot + 1 if slot == 4 else slot + 2)
+            d_re, d_im = image_ref[0, index], image_ref[1, index]
+            products.append((s_re * d_re - s_im * d_im, s_re * d_im + s_im * d_re))
+        store_halves(line_ref, c, 0, products[0][0])
+        store_halves(line_ref, c, 1, products[0][1])
+        store_halves(line_ref, c, 2, join(*products[1]))
+    spectra = along_y(line_ref, table_ref)
+    for pair in range(coils // 2):
+        first, second = (spectra[c * HALF : (c + 1) * HALF] for c in (2 * pair, 2 * pair + 1))
+        mixes = first[:, 2 * LANES :], second[:, 2 * LANES :]
+        for part, join_part in enumerate((join_low, join_high)):
+            columns = (
+                first[:, part * LANES : (part + 1) * LANES],
+                second[:, part * LANES : (part + 1) * LANES],
+                join_part(*mixes),
+            )
+            for column, value in enumerate(columns):
+                for term, half in enumerate(halves(value)):
+                    rows = slice(part * HALF, (part + 1) * HALF)
+                    mid_ref[term, pair, rows, column * LANES : (column + 1) * LANES] = half
+
+
+def first_kernel(recv_ref, first_ref, fwd_y_ref, mid_ref, line_ref):
+    forward_y(recv_ref, 0, first_ref, fwd_y_ref, line_ref, mid_ref)
 
 
 def normal_kernel(
     core_ref,
     recv_ref,
-    own_image_ref,
-    other_image_ref,
+    own_rest_ref,
+    other_rest_ref,
+    first_mid_ref,
     weight_ref,
     fwd_y_ref,
     inv_y_ref,
@@ -160,63 +205,29 @@
     def load(c, slot):
         return load_rows(recv_ref, c, slot)
 
-    image_ref[core] = own_image_ref[0]
-    image_ref[1 - core] = other_image_ref[0]
-
-    def store_line(row, c, column, value):
-        for term, half in enumerate(halves(value)):
-            at = (term * 3 + column) * LANES
-            line_ref[row, c * HALF : (c + 1) * HALF, at : at + LANES] = half
-
-    def along_y(row, table_ref):
-        twice = jnp.concatenate([table_ref[0], table_ref[0]], axis=0)
-        return dot(line_ref[row], twice) + dot(line_ref[row, :, : 3 * LANES], table_ref[1])
-
-    for c in range(coils):
-        for slot in range(3):
-            s_re = load(c, slot if slot < 2 else 4)
-            s_im = load(c, slot + 2 if slot < 2 else 5)
-            d_re, d_im = image_ref[0, slot], image_ref[1, slot]
-            x_re = s_re * d_re - s_im * d_im
-            x_im = s_re * d_im + s_im * d_re
-            if slot < 2:
-                store_line(slot, c, 0, x_re)
-                store_line(slot, c, 1, x_im)
-            else:
-                store_line(0, c, 2, join_low(x_re, x_im))
-                store_line(1, c, 2, join_high(x_re, x_im))
-    for row in range(2):
-        spectra = along_y(row, fwd_y_ref)
-        for pair in range(coils // 2):
-            first, second = (spectra[c * HALF : (c + 1) * HALF] for c in (2 * pair, 2 * pair + 1))
-            mixes = first[:, 2 * LANES :], second[:, 2 * LANES :]
-            for part, join in enumerate((join_low, join_high)):
-                at = (2 * part + row) * HALF
-                columns = (
-                    first[:, part * LANES : (part + 1) * LANES],
-                    second[:, part * LANES : (part + 1) * LANES],
-                    join(*mixes),
-                )
-                for column, value in enumerate(columns):
-                    for term, half in enumerate(halves(value)):
-                        mid_ref[term, pair, at : at + HALF, column * LANES : (column + 1) * LANES] = half
+    for part, rest_ref in ((core, own_rest_ref), (1 - core, other_rest_ref)):
+        image_ref[part, 0] = rest_ref[0]
+        image_ref[part, 1] = rest_ref[4]
+    forward_y(recv_ref, 1, image_ref, fwd_y_ref, line_ref.at[1], mid_ref)
     weight_low = weight_ref[:LANES].astype(jnp.float32).T
     weight_high = weight_ref[LANES:].astype(jnp.float32).T
     weight = jnp.concatenate([weight_low, weight_low, jnp.concatenate([weight_high, weight_high], axis=1)], axis=1)
     weight = jnp.concatenate([weight, weight], axis=0)
     for pair in range(coils // 2):
-        high, low = mid_ref[0, pair], mid_ref[1, pair]
+        high, low = (jnp.concatenate([first_mid_ref[term, pair], mid_ref[term, pair]], axis=0) for term in range(2))
         spectra = dot(fwd_x_ref[0], high) + (dot(fwd_x_ref[0], low) + dot(fwd_x_ref[1], high))
         high, low = halves(spectra * weight)
         value = dot(inv_x_ref[0], high) + (dot(inv_x_ref[0], low) + dot(inv_x_ref[1], high))
         for row in range(2):
-            re, im = (value[(2 * part + row) * HALF : (2 * part + row + 1) * HALF] for part in range(2))
+            re, im = (value[(2 * row + part) * HALF : (2 * row + part + 1) * HALF] for part in range(2))
             mixes = re[:, 2 * LANES :], im[:, 2 * LANES :]
             for index, join in enumerate((join_low, join_high)):
-                store_line(row, 2 * pair + index, 0, re[:, index * LANES : (index + 1) * LANES])
-                store_line(row, 2 * pair + index, 1, im[:, index * LANES : (index + 1) * LANES])
-                store_line(row, 2 * pair + index, 2, join(*mixes))
-    lines = [along_y(row, inv_y_ref) for row in range(2)]
+                columns = re, im
+                for column, value_part in enumerate(columns):
+                    lanes = slice(index * LANES, (index + 1) * LANES)
+                    store_halves(line_ref.at[row], 2 * pair + index, column, value_part[:, lanes])
+                store_halves(line_ref.at[row], 2 * pair + index, 2, join(*mixes))
+    lines = [along_y(line_ref.at[row], inv_y_ref) for row in range(2)]
     for slot in range(3):
         sum_re = jnp.zeros((HALF, LANES), jnp.float32)
         sum_im = jnp.zeros((HALF, LANES), jnp.float32)
@@ -235,13 +246,20 @@
         total_ref[1, slot] = sum_im
 
 
-def finish_kernel(core_ref, own_ref, other_ref, own_image_ref, other_image_ref, out_ref, total_ref):
+def finish_kernel(core_ref, own_ref, other_ref, first_ref, own_rest_ref, other_rest_ref, out_ref, total_ref):
     core = core_ref[0]
     part_sums = []
-    for part, image_ref in ((core, own_image_ref), (1 - core, other_image_ref)):
+    below = lane_index(HALF) < HALF
+    for part, rest_ref in ((core, own_rest_ref), (1 - core, other_rest_ref)):
         sums = [jnp.zeros((HALF, LANES), jnp.float32)] * 4
         for slot in range(3):
-            direction, residual = image_ref[0, slot], image_ref[1, slot]
+            residual = rest_ref[slot + 1]
+            if slot == 0:
+                direction = first_ref[part, 0]
+            elif slot == 1:
+                direction = rest_ref[0]
+            else:
+                direction = jnp.where(below, first_ref[part, 1], rest_ref[4])
             image_ap = own_ref[part, slot] + other_ref[part, slot] + damping_weight * direction
             total_ref[part, slot] = image_ap
             products = (residual * residual, direction * image_ap, residual * image_ap, image_ap * image_ap)
@@ -302,8 +320,8 @@
 def normal_scratch(planes):
     return [
         pltpu.VMEM((2, planes * HALF, 2 * 3 * LANES), jnp.bfloat16),
-        pltpu.VMEM((2, planes // 2, 2 * LANES, 3 * LANES), jnp.bfloat16),
-        pltpu.VMEM((2, 3, HALF, LANES), jnp.float32),
+        pltpu.VMEM((2, planes // 2, LANES, 3 * LANES), jnp.bfloat16),
+        pltpu.VMEM((2, 2, HALF, LANES), jnp.float32),
     ]
 
 
@@ -320,7 +338,7 @@
         in_specs=[hbm] * 3,
         out_shape=jax.ShapeDtypeStruct((devices * ROWS, LANES), f32),
         scratch_shapes=[pltpu.VMEM(a.shape, f32) for a in (sens_maps, direction, residual)]
-        + [pltpu.SemaphoreType.DMA((2, 2, 2)), pltpu.SemaphoreType.DMA((2,))],
+        + [pltpu.SemaphoreType.DMA((2,)), pltpu.SemaphoreType.DMA((2,))],
         compiler_params=params,
         name="pack",
     )(*(pltpu.with_memory_space_constraint(a, pltpu.HBM) for a in (sens_maps, direction, residual)))
@@ -331,27 +349,39 @@
     tables = [jnp.asarray(t) for t in make_tables(sampling.shape[1], sampling.shape[2])]
     swap = [(0, 1), (1, 0)]
     both = jax.ShapeDtypeStruct((2, 3, HALF, LANES), f32)
-    image = pl.pallas_call(image_kernel, out_shape=both, compiler_params=params, name="image")(moved)
-    other_image = lax.ppermute(image, "core", swap)
+    first, rest = pl.pallas_call(
+        image_kernel,
+        out_shape=(jax.ShapeDtypeStruct((2, 2, HALF, LANES), f32), jax.ShapeDtypeStruct((5, HALF, LANES), f32)),
+        compiler_params=params,
+        name="image",
+    )(moved)
+    other_rest = lax.ppermute(rest, "core", swap)
+    first_mid = pl.pallas_call(
+        first_kernel,
+        out_shape=jax.ShapeDtypeStruct((2, planes // 2, LANES, 3 * LANES), jnp.bfloat16),
+        scratch_shapes=[pltpu.VMEM((planes * HALF, 2 * 3 * LANES), jnp.bfloat16)],
+        compiler_params=params,
+        name="first",
+    )(moved, first, tables[0])
     scalar = pl.BlockSpec(memory_space=pltpu.SMEM)
     own = pl.pallas_call(
         normal_kernel,
-        in_specs=[scalar] + [whole] * (4 + len(tables)),
+        in_specs=[scalar] + [whole] * (5 + len(tables)),
         out_shape=both,
         scratch_shapes=normal_scratch(planes),
         compiler_params=params,
         name="normal",
-    )(core, moved, image, other_image, sampling[0].T, *tables)
+    )(core, moved, rest, other_rest, first_mid, sampling[0].T, *tables)
     other = lax.ppermute(own, "core", swap)
     chips = devices // 2
     result = pl.pallas_call(
         finish_kernel,
-        in_specs=[scalar] + [whole] * 4,
+        in_specs=[scalar] + [whole] * 5,
         out_shape=jax.ShapeDtypeStruct((chips, LANES), f32),
         scratch_shapes=[pltpu.VMEM(both.shape, f32)],
         compiler_params=params,
         name="finish",
-    )(core, own, other, image, other_image)
+    )(core, own, other, first, rest, other_rest)
     home = lax.all_to_all(result.reshape(chips, 1, LANES), ("coil", "chip"), 0, 0, tiled=True).reshape(chips, LANES)
     out = jax.ShapeDtypeStruct(direction.shape, f32)
     return tuple(

time: 111 us -> 110 us (level)
    pallas_call x3 -> x4, Pallas kernels: 5.84 us -> 6.22 us  [the longest x1 4.52 us: body(): pl.pallas_call(normal_kernel, in_specs=[scalar] + [whole] * (5 + len(tabl...]
  transfers between devices with their start and end apart: 2 -> 2, of which waited for: 2 -> 1; matrix products, arithmetic and copies ran while one was open for 0% -> 0% of each run, Pallas kernels for 0% -> 1%
where the time goes in v7:
time: 110 us
  blocking collectives  93 us (85%)
  Pallas kernels  8.91 us (8%)
  starting transfers between devices  5.74 us (5%)
    all_to_all x1, blocking collectives, body(): lax.all_to_all(packed.reshape(devices * ROWS, 1, LANES), axes, 0, 0, tile...  72.1 us
    all_to_all x1, blocking collectives, body(): lax.all_to_all(result.reshape(chips, 1, LANES), ('coil', 'chip'), 0, 0, t...  20.9 us
    pallas_call x1, Pallas kernels, body(): pl.pallas_call(normal_kernel, in_specs=[scalar] + [whole] * (5 + len(tabl...  4.52 us
    ppermute x1, starting transfers between devices, body(): other_rest = lax.ppermute(rest, 'core', swap)  3.48 us
    ppermute x1, starting transfers between devices, body(): other = lax.ppermute(own, 'core', swap)  2.26 us
  transfers between devices with their start and end apart: 2, of which 1 were waited for; matrix products, arithmetic and copies ran while one was open for 0% of the time, Pallas kernels for 1%

profile of v7, /device:TPU:1, one launch (start us, length us, event | category | flops | bytes accessed | tf_op | source)
XLA Modules:
  0.0 109.6 jit_solution(57143782958108467)
XLA Ops:
  0.6 1.8 %pack.1 = f32[3584,128]{1,0:T(8,128)S(1)} custom-call(f32[2,2,2,192,256]{4,3,2,1,0:T(8,128)} %maps_hbm.1, f32[2,1,2,24,256]{4,3,2,1,0:T(8,128)} %direction_ref.1, f32[2,1,2,24,256]{4,3,2,1,0:T(8,128)} %residual_ref.1), custom_call_target="tpu_custom_call" | custom-call | tf_op jit(solution)/shard_map/pack/pallas_call | solution.py:336
  2.5 72.1 %all_to_all.10 = f32[3584,1,128]{2,1,0:T(1,128)S(1)} all-to-all(f32[3584,1,128]{2,1,0:T(1,128)S(1)} %bitcast.15), channel_id=1, replica_groups=mesh['coil'=8,'chip'=32,'core'=2] {'coil','core','chip'}, dimensions={0} | all-to-all | bytes 3670016 | tf_op jit(solution)/shard_map/all_to_all | solution.py:347
  74.6 0.0 copy-start
  74.6 0.4 image.1
  75.0 0.0 copy-start.1
  75.0 0.0 copy-start.4
  75.0 0.0 copy-start.5
  75.0 0.0 copy-start.7
  75.0 3.5 %collective-permute-start = (f32[5,64,128]{2,1,0:T(8,128)S(1)}, f32[5,64,128]{2,1,0:T(8,128)S(1)}, u32[]{:S(2)}, u32[]{:S(2)}) collective-permute-start(f32[5,64,128]{2,1,0:T(8,128)S(1)} %get-tuple-element.9.own_rest_ref), channel_id=1, source_target_pairs={{0,1},{1,0},{2,3},{3,2},{4,5},{5,4},{6,7},{7,6},{8,9},{9,8},{10,11... | collective-permute-start | bytes 491528 | tf_op jit(solution)/shard_map/ppermute | solution.py:358
  78.5 0.0 copy-done
  78.5 1.0 first.1.first_mid_ref
  79.5 0.0 collective-permute-done.other_rest_ref
  79.5 0.0 copy-done.1
  79.5 0.0 copy-done.4
  79.5 0.0 copy-done.5
  79.6 0.0 copy-done.7
  79.6 0.0 copy-start.2
  79.6 0.0 copy-start.3
  79.6 0.0 copy-start.6
  79.6 4.5 %normal.1.own_ref = f32[2,3,64,128]{3,2,1,0:T(8,128)S(1)} custom-call(s32[1]{0:T(128)} %bitcast.core_ref, f32[3584,128]{1,0:T(8,128)S(1)} %bitcast.14, f32[5,64,128]{2,1,0:T(8,128)S(1)} %get-tuple-element.9.own_rest_ref, f32[5,64,128]{2,1,0:T(8,128)S(1)} %collective-permute-done.other_rest_ref, bf16[2,4,128,384]{3,2,1,0:T(8,128)(2,1)S(1)} %first.1.first_mid_ref, ...), custom_call_target="tpu_custom_call" | custom-call | tf_op jit(solution)/shard_map/normal/pallas_call | solution.py:367
  84.1 2.3 %collective-permute-start.1 = (f32[2,3,64,128]{3,2,1,0:T(8,128)S(1)}, f32[2,3,64,128]{3,2,1,0:T(8,128)S(1)}, u32[]{:S(2)}, u32[]{:S(2)}) collective-permute-start(f32[2,3,64,128]{3,2,1,0:T(8,128)S(1)} %normal.1.own_ref), channel_id=1, source_target_pairs={{0,1},{1,0},{2,3},{3,2},{4,5},{5,4},{6,7},{7,6},{8,9},{9,8},{10,11... | collective-permute-start | bytes 589832 | tf_op jit(solution)/shard_map/ppermute | solution.py:375
  86.4 1.1 collective-permute-done.1.other_ref
  87.5 0.3 finish.1
  87.8 20.9 %all_to_all.11 = f32[256,1,128]{2,1,0:T(1,128)S(1)} all-to-all(f32[256,1,128]{2,1,0:T(1,128)S(1)} %bitcast.16), channel_id=1, replica_groups=mesh['coil'=8,'chip'=32,'core'=2] {'coil','chip'}, dimensions={0} | all-to-all | bytes 262144 | tf_op jit(solution)/shard_map/all_to_all | solution.py:385
  108.7 0.0 copy-done.2
  108.7 0.0 copy-done.3
  108.7 0.0 copy-done.6
  108.7 0.8 update.1
Async XLA Ops:
  74.6 3.9 %copy-start = (bf16[2,384,384]{2,1,0:T(8,128)(2,1)S(1)}, bf16[2,384,384]{2,1,0:T(8,128)(2,1)}, u32[]{:S(2)}) copy-start(bf16[2,384,384]{2,1,0:T(8,128)(2,1)} %constant.12.clone.fwd_y_ref) | copy-start | bytes 1769476
  75.0 4.5 %copy-start.1 = (bf16[2,384,384]{2,1,0:T(8,128)(2,1)S(1)}, bf16[2,384,384]{2,1,0:T(8,128)(2,1)}, u32[]{:S(2)}) copy-start(bf16[2,384,384]{2,1,0:T(8,128)(2,1)} %constant.13.clone.inv_y_ref) | copy-start | bytes 1769476
  75.0 4.5 %copy-start.4 = (bf16[2,256,256]{2,1,0:T(8,128)(2,1)S(1)}, bf16[2,256,256]{2,1,0:T(8,128)(2,1)}, u32[]{:S(2)}) copy-start(bf16[2,256,256]{2,1,0:T(8,128)(2,1)} %constant.15.clone.inv_x_ref) | copy-start | bytes 786436
  75.0 4.5 %copy-start.5 = (bf16[2,256,256]{2,1,0:T(8,128)(2,1)S(1)}, bf16[2,256,256]{2,1,0:T(8,128)(2,1)}, u32[]{:S(2)}) copy-start(bf16[2,256,256]{2,1,0:T(8,128)(2,1)} %constant.14.clone.fwd_x_ref) | copy-start | bytes 786436
  75.0 4.5 %copy-start.7 = (s32[1,128,192]{1,2,0:T(8,128)S(1)}, s32[1,128,192]{1,2,0:T(8,128)}, u32[]{:S(2)}) copy-start(s32[1,128,192]{1,2,0:T(8,128)} %param.13) | copy-start | bytes 294916
  75.0 4.5 %collective-permute-start = (f32[5,64,128]{2,1,0:T(8,128)S(1)}, f32[5,64,128]{2,1,0:T(8,128)S(1)}, u32[]{:S(2)}, u32[]{:S(2)}) collective-permute-start(f32[5,64,128]{2,1,0:T(8,128)S(1)} %get-tuple-element.9.own_rest_ref), channel_id=1, source_target_pairs={{0,1},{1,0},{2,3},{3,2},{4,5},{5,4},{6,7},{7,6},{8,9},{9,8},{10,11... | collective-permute-start | bytes 491528 | tf_op jit(solution)/shard_map/ppermute | solution.py:358
  79.6 29.2 %copy-start.2 = (f32[2,1,2,24,256]{4,3,2,1,0:T(8,128)S(1)}, f32[2,1,2,24,256]{4,3,2,1,0:T(8,128)}, u32[]{:S(2)}) copy-start(f32[2,1,2,24,256]{4,3,2,1,0:T(8,128)} %direction_ref.1) | copy-start | bytes 294916
  79.6 29.2 %copy-start.3 = (f32[2,1,2,24,256]{4,3,2,1,0:T(8,128)S(1)}, f32[2,1,2,24,256]{4,3,2,1,0:T(8,128)}, u32[]{:S(2)}) copy-start(f32[2,1,2,24,256]{4,3,2,1,0:T(8,128)} %residual_ref.1) | copy-start | bytes 294916
  79.6 29.1 %copy-start.6 = (f32[2,1,2,24,256]{4,3,2,1,0:T(8,128)S(1)}, f32[2,1,2,24,256]{4,3,2,1,0:T(8,128)}, u32[]{:S(2)}) copy-start(f32[2,1,2,24,256]{4,3,2,1,0:T(8,128)} %solution_ref.1) | copy-start | bytes 294916
  84.1 3.3 %collective-permute-start.1 = (f32[2,3,64,128]{3,2,1,0:T(8,128)S(1)}, f32[2,3,64,128]{3,2,1,0:T(8,128)S(1)}, u32[]{:S(2)}, u32[]{:S(2)}) collective-permute-start(f32[2,3,64,128]{3,2,1,0:T(8,128)S(1)} %normal.1.own_ref), channel_id=1, source_target_pairs={{0,1},{1,0},{2,3},{3,2},{4,5},{5,4},{6,7},{7,6},{8,9},{9,8},{10,11... | collective-permute-start | bytes 589832 | tf_op jit(solution)/shard_map/ppermute | solution.py:375

commit v8 on v7

--- a/solution.py
+++ b/solution.py
@@ -17,6 +17,7 @@
 MESSAGE_IMAGE = 6
 HALF = 64
 QUARTER = 32
+EIGHT = 8
 SUMS_AT = 96
 
 
@@ -39,7 +40,7 @@
     re_from_re = np.concatenate([cos_y[:, :LANES], -sin_y[:, :LANES], cos_y[:, LANES:], -sin_y[:, LANES:]], axis=1)
     re_from_im = np.concatenate([sin_y[:, :LANES], cos_y[:, :LANES], sin_y[:, LANES:], cos_y[:, LANES:]], axis=1)
     fwd_y = np.concatenate([re_from_re[:LANES], re_from_im[:LANES], re_from_re[LANES:], re_from_im[LANES:]], axis=0)
-    order = np.arange(size_x).reshape(-1, 2, 2).transpose(2, 1, 0).reshape(-1)
+    order = np.arange(size_x).reshape(EIGHT, -1, 2, 2).transpose(3, 0, 2, 1).reshape(-1)
     fwd_x = np.block([[cos_x[:, order], sin_x[:, order]], [-sin_x[:, order], cos_x[:, order]]])
     fwd_x = fwd_x.reshape(2 * size_x, 2, 2, HALF).transpose(0, 2, 1, 3).reshape(2 * size_x, 2 * size_x)
     return [split_pair(t) for t in (fwd_y, fwd_y.T, fwd_x, fwd_x.T)]
@@ -59,9 +60,9 @@
 
     def put(core, slot, block):
         turned = block.T
-        for plane in range(cells // QUARTER):
-            rows = pl.ds((plane * HALF + core * QUARTER) * ROWS + slot, QUARTER, stride=ROWS)
-            out_ref[rows, :] = turned[plane * QUARTER : (plane + 1) * QUARTER]
+        for place in range(4):
+            rows = pl.ds((core * 4 + place) * ROWS + slot, cells // 4, stride=EIGHT * ROWS)
+            out_ref[rows, :] = turned[place * (cells // 4) : (place + 1) * (cells // 4)]
 
     for core in range(2):
         copies[core].wait()
@@ -123,7 +124,8 @@
 
 
 def load_rows(recv_ref, c, slot):
-    return recv_ref[pl.ds(c * HALF * ROWS + slot, HALF, stride=ROWS), :]
+    starts = ((line * EIGHT + c) * EIGHT * ROWS + slot for line in range(EIGHT))
+    return jnp.concatenate([recv_ref[pl.ds(start, EIGHT, stride=ROWS), :] for start in starts], axis=0)
 
 
 def image_kernel(recv_ref, first_ref, rest_ref):
@@ -261,7 +263,7 @@
             else:
                 direction = jnp.where(below, first_ref[part, 1], rest_ref[4])
             image_ap = own_ref[part, slot] + other_ref[part, slot] + damping_weight * direction
-            total_ref[part, slot] = image_ap
+            total_ref[pl.ds(pl.multiple_of((part * 3 + slot) * HALF, HALF), HALF), :] = image_ap
             products = (residual * residual, direction * image_ap, residual * image_ap, image_ap * image_ap)
             sums = [a + b for a, b in zip(sums, products)]
         part_sums.append(sums)
@@ -272,8 +274,18 @@
         message = jnp.where(lane == SUMS_AT + index, jnp.sum(product), message)
     planes = out_ref.shape[0] // QUARTER
     own = 2 * 96 // planes
-    rows = pl.ds(pl.multiple_of(core * QUARTER, QUARTER), QUARTER)
-    lines = [[total_ref[part, slot, rows, :] for slot in range(3)] for part in range(2)]
+
+    def owned(part, slot):
+        base = (part * 3 + slot) * HALF
+        first, second = (
+            jnp.concatenate(
+                [total_ref[pl.ds(base + index * 4 + place, EIGHT, stride=EIGHT), :] for place in range(4)], axis=0
+            )
+            for index in range(2)
+        )
+        return jnp.where(core == 0, first, second)
+
+    lines = [[owned(part, slot) for slot in range(3)] for part in range(2)]
     for c in range(planes):
         start = c * own
         block = message
@@ -288,7 +300,8 @@
                     if start < LANES:
                         inside = inside & (lane >= at + LANES - start)
                     block = jnp.where(inside, moved, block)
-        out_ref[c * QUARTER : (c + 1) * QUARTER, :] = block
+        for place in range(4):
+            out_ref[pl.ds(place * HALF + c, EIGHT, stride=EIGHT), :] = block[place * EIGHT : (place + 1) * EIGHT]
 
 
 def update_kernel(
@@ -326,7 +339,8 @@
 
 
 def body(solution, residual, direction, sens_maps, sampling):
-    axes = ("coil", "core", "chip")
+    chip_axes = ("place", "line", "coil")
+    axes = ("line", "coil", "core", "place")
     devices = lax.axis_size(axes)
     planes = lax.axis_size("coil")
     f32 = jnp.float32
@@ -378,11 +392,11 @@
         finish_kernel,
         in_specs=[scalar] + [whole] * 5,
         out_shape=jax.ShapeDtypeStruct((chips, LANES), f32),
-        scratch_shapes=[pltpu.VMEM(both.shape, f32)],
+        scratch_shapes=[pltpu.VMEM((2 * 3 * HALF, LANES), f32)],
         compiler_params=params,
         name="finish",
     )(core, own, other, first, rest, other_rest)
-    home = lax.all_to_all(result.reshape(chips, 1, LANES), ("coil", "chip"), 0, 0, tiled=True).reshape(chips, LANES)
+    home = lax.all_to_all(result.reshape(chips, 1, LANES), chip_axes, 0, 0, tiled=True).reshape(chips, LANES)
     out = jax.ShapeDtypeStruct(direction.shape, f32)
     return tuple(
         pl.pallas_call(update_kernel, out_shape=(out, out, out), compiler_params=params, name="update")(
@@ -392,8 +406,8 @@
 
 
 def solution(mesh):
-    planes, slabs = mesh.devices.shape
-    split = Mesh(mesh.devices.reshape(planes, slabs // 2, 2), ("coil", "chip", "core"))
-    image = P(None, None, ("chip", "core"), "coil", None)
-    in_specs = (image, image, image, P(None, "coil", ("chip", "core"), None, None), P())
+    split = Mesh(mesh.devices.reshape(mesh.devices.shape[0], EIGHT, -1, 2), ("coil", "line", "place", "core"))
+    slab = ("line", "place", "core")
+    image = P(None, None, slab, "coil", None)
+    in_specs = (image, image, image, P(None, "coil", slab, None, None), P())
     return jax.shard_map(body, mesh=split, in_specs=in_specs, out_specs=(image, image, image), check_vma=False)

time: 110 us -> 110 us (level)
  starting transfers between devices: 5.74 us -> 4.16 us
    all_to_all x1, blocking collectives: 20.9 us -> 23 us  [body(): lax.all_to_all(result.reshape(chips, 1, LANES), chip_axes, 0, 0, tiled=True)]
    all_to_all x1, blocking collectives: 72.1 us -> 70.5 us  [body(): lax.all_to_all(packed.reshape(devices * ROWS, 1, LANES), axes, 0, 0, tile...]
    ppermute x1, starting transfers between devices: 3.48 us -> 2.1 us  [body(): other_rest = lax.ppermute(rest, 'core', swap)]
  transfers between devices with their start and end apart: 2 -> 2, of which waited for: 1 -> 2; matrix products, arithmetic and copies ran while one was open for 0% -> 0% of each run, Pallas kernels for 1% -> 1%
where the time goes in v8:
time: 110 us; the launch traced here: 109 us
  blocking collectives  93.5 us (85%)
  Pallas kernels  8.9 us (8%)
  starting transfers between devices  4.16 us (4%)
  waiting for transfers between devices  1.6 us (1%)
    all_to_all x1, blocking collectives, body(): lax.all_to_all(packed.reshape(devices * ROWS, 1, LANES), axes, 0, 0, tile...  70.5 us
    all_to_all x1, blocking collectives, body(): lax.all_to_all(result.reshape(chips, 1, LANES), chip_axes, 0, 0, tiled=True)  23 us
    pallas_call x1, Pallas kernels, body(): pl.pallas_call(normal_kernel, in_specs=[scalar] + [whole] * (5 + len(tabl...  4.51 us
  transfers between devices with their start and end apart: 2, of which 2 were waited for; matrix products, arithmetic and copies ran while one was open for 0% of the time, Pallas kernels for 1%

profile of v8, /device:TPU:1, one launch (start us, length us, event | category | flops | bytes accessed | tf_op | source)
XLA Modules:
  0.0 109.0 jit_solution(4966358160640971957)
XLA Ops:
  0.6 1.8 %pack.1 = f32[3584,128]{1,0:T(8,128)S(1)} custom-call(f32[2,2,2,192,256]{4,3,2,1,0:T(8,128)} %maps_hbm.1, f32[2,1,2,24,256]{4,3,2,1,0:T(8,128)} %direction_ref.1, f32[2,1,2,24,256]{4,3,2,1,0:T(8,128)} %residual_ref.1), custom_call_target="tpu_custom_call" | custom-call | tf_op jit(solution)/shard_map/pack/pallas_call | solution.py:350
  2.5 70.5 %all_to_all.10 = f32[3584,1,128]{2,1,0:T(1,128)S(1)} all-to-all(f32[3584,1,128]{2,1,0:T(1,128)S(1)} %bitcast.15), channel_id=1, replica_groups=mesh['coil'=8,'line'=8,'place'=4,'core'=2] {'line','coil','core','place'}, dimensions={0} | all-to-all | bytes 3670016 | tf_op jit(solution)/shard_map/all_to_all | solution.py:361
  73.0 0.0 copy-start
  73.0 0.4 image.1
  73.4 0.0 copy-start.1
  73.5 0.0 copy-start.4
  73.5 0.0 copy-start.5
  73.5 0.0 copy-start.7
  73.5 2.1 %collective-permute-start = (f32[5,64,128]{2,1,0:T(8,128)S(1)}, f32[5,64,128]{2,1,0:T(8,128)S(1)}, u32[]{:S(2)}, u32[]{:S(2)}) collective-permute-start(f32[5,64,128]{2,1,0:T(8,128)S(1)} %get-tuple-element.9.own_rest_ref), channel_id=1, source_target_pairs={{0,1},{1,0},{2,3},{3,2},{4,5},{5,4},{6,7},{7,6},{8,9},{9,8},{10,11... | collective-permute-start | bytes 491528 | tf_op jit(solution)/shard_map/ppermute | solution.py:372
  75.6 0.0 copy-done
  75.6 1.0 first.1.first_mid_ref
  76.6 0.3 collective-permute-done.other_rest_ref
  76.9 0.0 copy-done.1
  76.9 0.0 copy-done.4
  76.9 0.0 copy-done.5
  76.9 0.0 copy-done.7
  76.9 0.0 copy-start.2
  77.0 0.0 copy-start.3
  77.0 0.0 copy-start.6
  77.0 4.5 %normal.1.own_ref = f32[2,3,64,128]{3,2,1,0:T(8,128)S(1)} custom-call(s32[1]{0:T(128)} %bitcast.core_ref, f32[3584,128]{1,0:T(8,128)S(1)} %bitcast.14, f32[5,64,128]{2,1,0:T(8,128)S(1)} %get-tuple-element.9.own_rest_ref, f32[5,64,128]{2,1,0:T(8,128)S(1)} %collective-permute-done.other_rest_ref, bf16[2,4,128,384]{3,2,1,0:T(8,128)(2,1)S(1)} %first.1.first_mid_ref, ...), custom_call_target="tpu_custom_call" | custom-call | tf_op jit(solution)/shard_map/normal/pallas_call | solution.py:381
  81.5 2.1 %collective-permute-start.1 = (f32[2,3,64,128]{3,2,1,0:T(8,128)S(1)}, f32[2,3,64,128]{3,2,1,0:T(8,128)S(1)}, u32[]{:S(2)}, u32[]{:S(2)}) collective-permute-start(f32[2,3,64,128]{3,2,1,0:T(8,128)S(1)} %normal.1.own_ref), channel_id=1, source_target_pairs={{0,1},{1,0},{2,3},{3,2},{4,5},{5,4},{6,7},{7,6},{8,9},{9,8},{10,11... | collective-permute-start | bytes 589832 | tf_op jit(solution)/shard_map/ppermute | solution.py:389
  83.6 1.3 %collective-permute-done.1.other_ref = f32[2,3,64,128]{3,2,1,0:T(8,128)S(1)} collective-permute-done((f32[2,3,64,128]{3,2,1,0:T(8,128)S(1)}, f32[2,3,64,128]{3,2,1,0:T(8,128)S(1)}, u32[]{:S(2)}, u32[]{:S(2)}) %collective-permute-start.1) | collective-permute-done | bytes 196640 | tf_op jit(solution)/shard_map/ppermute | solution.py:389
  84.8 0.3 finish.1
  85.2 23.0 %all_to_all.11 = f32[256,1,128]{2,1,0:T(1,128)S(1)} all-to-all(f32[256,1,128]{2,1,0:T(1,128)S(1)} %bitcast.16), channel_id=1, replica_groups=mesh['coil'=8,'line'=8,'place'=4,'core'=2] {'place','line','coil'}, dimensions={0} | all-to-all | bytes 262144 | tf_op jit(solution)/shard_map/all_to_all | solution.py:399
  108.1 0.0 copy-done.2
  108.1 0.0 copy-done.3
  108.1 0.0 copy-done.6
  108.1 0.8 update.1
Async XLA Ops:
  73.0 2.6 %copy-start = (bf16[2,384,384]{2,1,0:T(8,128)(2,1)S(1)}, bf16[2,384,384]{2,1,0:T(8,128)(2,1)}, u32[]{:S(2)}) copy-start(bf16[2,384,384]{2,1,0:T(8,128)(2,1)} %constant.12.clone.fwd_y_ref) | copy-start | bytes 1769476
  73.4 3.5 %copy-start.1 = (bf16[2,384,384]{2,1,0:T(8,128)(2,1)S(1)}, bf16[2,384,384]{2,1,0:T(8,128)(2,1)}, u32[]{:S(2)}) copy-start(bf16[2,384,384]{2,1,0:T(8,128)(2,1)} %constant.13.clone.inv_y_ref) | copy-start | bytes 1769476
  73.5 3.5 %copy-start.4 = (bf16[2,256,256]{2,1,0:T(8,128)(2,1)S(1)}, bf16[2,256,256]{2,1,0:T(8,128)(2,1)}, u32[]{:S(2)}) copy-start(bf16[2,256,256]{2,1,0:T(8,128)(2,1)} %constant.15.clone.inv_x_ref) | copy-start | bytes 786436
  73.5 3.5 %copy-start.5 = (bf16[2,256,256]{2,1,0:T(8,128)(2,1)S(1)}, bf16[2,256,256]{2,1,0:T(8,128)(2,1)}, u32[]{:S(2)}) copy-start(bf16[2,256,256]{2,1,0:T(8,128)(2,1)} %constant.14.clone.fwd_x_ref) | copy-start | bytes 786436
  73.5 3.4 %copy-start.7 = (s32[1,128,192]{1,2,0:T(8,128)S(1)}, s32[1,128,192]{1,2,0:T(8,128)}, u32[]{:S(2)}) copy-start(s32[1,128,192]{1,2,0:T(8,128)} %param.13) | copy-start | bytes 294916
  73.5 3.4 %collective-permute-start = (f32[5,64,128]{2,1,0:T(8,128)S(1)}, f32[5,64,128]{2,1,0:T(8,128)S(1)}, u32[]{:S(2)}, u32[]{:S(2)}) collective-permute-start(f32[5,64,128]{2,1,0:T(8,128)S(1)} %get-tuple-element.9.own_rest_ref), channel_id=1, source_target_pairs={{0,1},{1,0},{2,3},{3,2},{4,5},{5,4},{6,7},{7,6},{8,9},{9,8},{10,11... | collective-permute-start | bytes 491528 | tf_op jit(solution)/shard_map/ppermute | solution.py:372
  76.9 31.2 %copy-start.2 = (f32[2,1,2,24,256]{4,3,2,1,0:T(8,128)S(1)}, f32[2,1,2,24,256]{4,3,2,1,0:T(8,128)}, u32[]{:S(2)}) copy-start(f32[2,1,2,24,256]{4,3,2,1,0:T(8,128)} %direction_ref.1) | copy-start | bytes 294916
  77.0 31.2 %copy-start.3 = (f32[2,1,2,24,256]{4,3,2,1,0:T(8,128)S(1)}, f32[2,1,2,24,256]{4,3,2,1,0:T(8,128)}, u32[]{:S(2)}) copy-start(f32[2,1,2,24,256]{4,3,2,1,0:T(8,128)} %residual_ref.1) | copy-start | bytes 294916
  77.0 31.2 %copy-start.6 = (f32[2,1,2,24,256]{4,3,2,1,0:T(8,128)S(1)}, f32[2,1,2,24,256]{4,3,2,1,0:T(8,128)}, u32[]{:S(2)}) copy-start(f32[2,1,2,24,256]{4,3,2,1,0:T(8,128)} %solution_ref.1) | copy-start | bytes 294916
  81.5 3.3 %collective-permute-start.1 = (f32[2,3,64,128]{3,2,1,0:T(8,128)S(1)}, f32[2,3,64,128]{3,2,1,0:T(8,128)S(1)}, u32[]{:S(2)}, u32[]{:S(2)}) collective-permute-start(f32[2,3,64,128]{3,2,1,0:T(8,128)S(1)} %normal.1.own_ref), channel_id=1, source_target_pairs={{0,1},{1,0},{2,3},{3,2},{4,5},{5,4},{6,7},{7,6},{8,9},{9,8},{10,11... | collective-permute-start | bytes 589832 | tf_op jit(solution)/shard_map/ppermute | solution.py:389

commit v9 on v8

--- a/solution.py
+++ b/solution.py
@@ -301,7 +301,7 @@
                         inside = inside & (lane >= at + LANES - start)
                     block = jnp.where(inside, moved, block)
         for place in range(4):
-            out_ref[pl.ds(place * HALF + c, EIGHT, stride=EIGHT), :] = block[place * EIGHT : (place + 1) * EIGHT]
+            out_ref[pl.ds(c * QUARTER + place, EIGHT, stride=4), :] = block[place * EIGHT : (place + 1) * EIGHT]
 
 
 def update_kernel(
@@ -318,7 +318,8 @@
     alpha = norm_now / curvature
     fresh = jnp.maximum(norm_now + alpha * (alpha * square - 2.0 * cross), 0.0)
     beta = fresh / norm_now
-    turned = recv_ref[...].T
+    starts = (line * 4 + place for place in range(4) for line in range(EIGHT))
+    turned = jnp.concatenate([recv_ref[pl.ds(start, EIGHT, stride=QUARTER), :] for start in starts], axis=0).T
     for part in range(2):
         for row in range(2):
             at = (2 * part + row) * own
@@ -339,7 +340,7 @@
 
 
 def body(solution, residual, direction, sens_maps, sampling):
-    chip_axes = ("place", "line", "coil")
+    chip_axes = ("coil", "line", "place")
     axes = ("line", "coil", "core", "place")
     devices = lax.axis_size(axes)
     planes = lax.axis_size("coil")

time: 110 us -> 109 us (level); the launches traced: 109 us -> 109 us
  no operation moved by 1% of the time
where the time goes in v9:
time: 109 us
  blocking collectives  93.6 us (86%)
  Pallas kernels  8.91 us (8%)
  starting transfers between devices  4.16 us (4%)
  waiting for transfers between devices  1.6 us (1%)
    all_to_all x1, blocking collectives, body(): lax.all_to_all(packed.reshape(devices * ROWS, 1, LANES), axes, 0, 0, tile...  70.5 us
    all_to_all x1, blocking collectives, body(): lax.all_to_all(result.reshape(chips, 1, LANES), chip_axes, 0, 0, tiled=True)  23.1 us
    pallas_call x1, Pallas kernels, body(): pl.pallas_call(normal_kernel, in_specs=[scalar] + [whole] * (5 + len(tabl...  4.51 us
  transfers between devices with their start and end apart: 2, of which 2 were waited for; matrix products, arithmetic and copies ran while one was open for 0% of the time, Pallas kernels for 1%

profile of v9, /device:TPU:1, one launch (start us, length us, event | category | flops | bytes accessed | tf_op | source)
XLA Modules:
  0.0 109.1 jit_solution(1680563794241355111)
XLA Ops:
  0.6 1.8 %pack.1 = f32[3584,128]{1,0:T(8,128)S(1)} custom-call(f32[2,2,2,192,256]{4,3,2,1,0:T(8,128)} %maps_hbm.1, f32[2,1,2,24,256]{4,3,2,1,0:T(8,128)} %direction_ref.1, f32[2,1,2,24,256]{4,3,2,1,0:T(8,128)} %residual_ref.1), custom_call_target="tpu_custom_call" | custom-call | tf_op jit(solution)/shard_map/pack/pallas_call | solution.py:351
  2.5 70.5 %all_to_all.10 = f32[3584,1,128]{2,1,0:T(1,128)S(1)} all-to-all(f32[3584,1,128]{2,1,0:T(1,128)S(1)} %bitcast.15), channel_id=1, replica_groups=mesh['coil'=8,'line'=8,'place'=4,'core'=2] {'line','coil','core','place'}, dimensions={0} | all-to-all | bytes 3670016 | tf_op jit(solution)/shard_map/all_to_all | solution.py:362
  73.0 0.0 copy-start
  73.0 0.4 image.1
  73.4 0.0 copy-start.1
  73.5 0.0 copy-start.4
  73.5 0.0 copy-start.5
  73.5 0.0 copy-start.7
  73.5 2.1 %collective-permute-start = (f32[5,64,128]{2,1,0:T(8,128)S(1)}, f32[5,64,128]{2,1,0:T(8,128)S(1)}, u32[]{:S(2)}, u32[]{:S(2)}) collective-permute-start(f32[5,64,128]{2,1,0:T(8,128)S(1)} %get-tuple-element.9.own_rest_ref), channel_id=1, source_target_pairs={{0,1},{1,0},{2,3},{3,2},{4,5},{5,4},{6,7},{7,6},{8,9},{9,8},{10,11... | collective-permute-start | bytes 491528 | tf_op jit(solution)/shard_map/ppermute | solution.py:373
  75.6 0.0 copy-done
  75.6 1.0 first.1.first_mid_ref
  76.6 0.3 collective-permute-done.other_rest_ref
  76.9 0.0 copy-done.1
  76.9 0.0 copy-done.4
  76.9 0.0 copy-done.5
  76.9 0.0 copy-done.7
  76.9 0.0 copy-start.2
  77.0 0.0 copy-start.3
  77.0 0.0 copy-start.6
  77.0 4.5 %normal.1.own_ref = f32[2,3,64,128]{3,2,1,0:T(8,128)S(1)} custom-call(s32[1]{0:T(128)} %bitcast.core_ref, f32[3584,128]{1,0:T(8,128)S(1)} %bitcast.14, f32[5,64,128]{2,1,0:T(8,128)S(1)} %get-tuple-element.9.own_rest_ref, f32[5,64,128]{2,1,0:T(8,128)S(1)} %collective-permute-done.other_rest_ref, bf16[2,4,128,384]{3,2,1,0:T(8,128)(2,1)S(1)} %first.1.first_mid_ref, ...), custom_call_target="tpu_custom_call" | custom-call | tf_op jit(solution)/shard_map/normal/pallas_call | solution.py:382
  81.5 2.1 %collective-permute-start.1 = (f32[2,3,64,128]{3,2,1,0:T(8,128)S(1)}, f32[2,3,64,128]{3,2,1,0:T(8,128)S(1)}, u32[]{:S(2)}, u32[]{:S(2)}) collective-permute-start(f32[2,3,64,128]{3,2,1,0:T(8,128)S(1)} %normal.1.own_ref), channel_id=1, source_target_pairs={{0,1},{1,0},{2,3},{3,2},{4,5},{5,4},{6,7},{7,6},{8,9},{9,8},{10,11... | collective-permute-start | bytes 589832 | tf_op jit(solution)/shard_map/ppermute | solution.py:390
  83.6 1.3 %collective-permute-done.1.other_ref = f32[2,3,64,128]{3,2,1,0:T(8,128)S(1)} collective-permute-done((f32[2,3,64,128]{3,2,1,0:T(8,128)S(1)}, f32[2,3,64,128]{3,2,1,0:T(8,128)S(1)}, u32[]{:S(2)}, u32[]{:S(2)}) %collective-permute-start.1) | collective-permute-done | bytes 196640 | tf_op jit(solution)/shard_map/ppermute | solution.py:390
  84.8 0.3 finish.1
  85.2 23.1 %all_to_all.11 = f32[256,1,128]{2,1,0:T(1,128)S(1)} all-to-all(f32[256,1,128]{2,1,0:T(1,128)S(1)} %bitcast.16), channel_id=1, replica_groups=mesh['coil'=8,'line'=8,'place'=4,'core'=2] {'coil','line','place'}, dimensions={0} | all-to-all | bytes 262144 | tf_op jit(solution)/shard_map/all_to_all | solution.py:400
  108.2 0.0 copy-done.2
  108.2 0.0 copy-done.3
  108.2 0.0 copy-done.6
  108.2 0.9 update.1
Async XLA Ops:
  73.0 2.6 %copy-start = (bf16[2,384,384]{2,1,0:T(8,128)(2,1)S(1)}, bf16[2,384,384]{2,1,0:T(8,128)(2,1)}, u32[]{:S(2)}) copy-start(bf16[2,384,384]{2,1,0:T(8,128)(2,1)} %constant.12.clone.fwd_y_ref) | copy-start | bytes 1769476
  73.4 3.5 %copy-start.1 = (bf16[2,384,384]{2,1,0:T(8,128)(2,1)S(1)}, bf16[2,384,384]{2,1,0:T(8,128)(2,1)}, u32[]{:S(2)}) copy-start(bf16[2,384,384]{2,1,0:T(8,128)(2,1)} %constant.13.clone.inv_y_ref) | copy-start | bytes 1769476
  73.5 3.5 %copy-start.4 = (bf16[2,256,256]{2,1,0:T(8,128)(2,1)S(1)}, bf16[2,256,256]{2,1,0:T(8,128)(2,1)}, u32[]{:S(2)}) copy-start(bf16[2,256,256]{2,1,0:T(8,128)(2,1)} %constant.15.clone.inv_x_ref) | copy-start | bytes 786436
  73.5 3.5 %copy-start.5 = (bf16[2,256,256]{2,1,0:T(8,128)(2,1)S(1)}, bf16[2,256,256]{2,1,0:T(8,128)(2,1)}, u32[]{:S(2)}) copy-start(bf16[2,256,256]{2,1,0:T(8,128)(2,1)} %constant.14.clone.fwd_x_ref) | copy-start | bytes 786436
  73.5 3.4 %copy-start.7 = (s32[1,128,192]{1,2,0:T(8,128)S(1)}, s32[1,128,192]{1,2,0:T(8,128)}, u32[]{:S(2)}) copy-start(s32[1,128,192]{1,2,0:T(8,128)} %param.13) | copy-start | bytes 294916
  73.5 3.4 %collective-permute-start = (f32[5,64,128]{2,1,0:T(8,128)S(1)}, f32[5,64,128]{2,1,0:T(8,128)S(1)}, u32[]{:S(2)}, u32[]{:S(2)}) collective-permute-start(f32[5,64,128]{2,1,0:T(8,128)S(1)} %get-tuple-element.9.own_rest_ref), channel_id=1, source_target_pairs={{0,1},{1,0},{2,3},{3,2},{4,5},{5,4},{6,7},{7,6},{8,9},{9,8},{10,11... | collective-permute-start | bytes 491528 | tf_op jit(solution)/shard_map/ppermute | solution.py:373
  76.9 31.3 %copy-start.2 = (f32[2,1,2,24,256]{4,3,2,1,0:T(8,128)S(1)}, f32[2,1,2,24,256]{4,3,2,1,0:T(8,128)}, u32[]{:S(2)}) copy-start(f32[2,1,2,24,256]{4,3,2,1,0:T(8,128)} %direction_ref.1) | copy-start | bytes 294916
  77.0 31.3 %copy-start.3 = (f32[2,1,2,24,256]{4,3,2,1,0:T(8,128)S(1)}, f32[2,1,2,24,256]{4,3,2,1,0:T(8,128)}, u32[]{:S(2)}) copy-start(f32[2,1,2,24,256]{4,3,2,1,0:T(8,128)} %residual_ref.1) | copy-start | bytes 294916
  77.0 31.3 %copy-start.6 = (f32[2,1,2,24,256]{4,3,2,1,0:T(8,128)S(1)}, f32[2,1,2,24,256]{4,3,2,1,0:T(8,128)}, u32[]{:S(2)}) copy-start(f32[2,1,2,24,256]{4,3,2,1,0:T(8,128)} %solution_ref.1) | copy-start | bytes 294916
  81.5 3.3 %collective-permute-start.1 = (f32[2,3,64,128]{3,2,1,0:T(8,128)S(1)}, f32[2,3,64,128]{3,2,1,0:T(8,128)S(1)}, u32[]{:S(2)}, u32[]{:S(2)}) collective-permute-start(f32[2,3,64,128]{3,2,1,0:T(8,128)S(1)} %normal.1.own_ref), channel_id=1, source_target_pairs={{0,1},{1,0},{2,3},{3,2},{4,5},{5,4},{6,7},{7,6},{8,9},{9,8},{10,11... | collective-permute-start | bytes 589832 | tf_op jit(solution)/shard_map/ppermute | solution.py:390
